TPU v7x, 128 devices: a whole 4x4x4 slice. The times are simulated.
128 devices in a mesh: row: 8 (over x, core), col: 16 (over y, z).
Axes of the slice: x: 4, y: 4, z: 4, core: 2. Of those that a mesh axis runs over, the one named last changes fastest.
Arguments:
- currents: float32 [32768, 256], P(('row', 'col')), may hold values from -6 to 6
- branch_owner: int32 [32768, 2], P(('row', 'col')), may hold values from 0 to 127, all different within a row; in each aligned block of 256 rows (0 to 255, 256 to 511, ...) at most 16 rows name the same one
- branch_slot: int32 [32768, 2], P(('row', 'col')), may hold values from 0 to 1023
- history: bfloat16 [4, 131072, 256], P(None, 'col'), may hold values from -6 to 6
- coefficients: bfloat16 [4096, 131072], P('row', 'col'), may hold values from -0.0234375 to 0.0234375
- delays: int32 [16, 512], P('row', 'col'), may hold values from 0 to 4
- slab_owner: int32 [8192, 2], P(('row', 'col')), may hold values from 0 to 127, all different within a row; in each aligned block of 64 rows (0 to 63, 64 to 127, ...) at most 4 rows name the same one
- slab_offset: int32 [8192, 2], P(('row', 'col')), may hold values from 0 to 31
Outputs:
- charge_now: bfloat16 [131072, 256], P('col')
- drops: float32 [8192, 256], P(('row', 'col'))
Inputs may be any that keep to these rules, and one draw needn't show every extreme that they name: `branch_owner`: the two ends of a branch have different owners; among the rows of one device no owner is named more than 16 times. `slab_owner`: the two ends of a slab branch have different owners; among the rows of one device no owner is named more than 4 times.
All inputs are finite; a program needn't handle non-finite values.
Results may differ from a plain program's by a relative error of at most 0.0015.
Values may be sent and summed in bfloat16 or wider, within the bound.
A program may use at most 128 MiB of HBM per device.

v0:
```python
import jax
import jax.numpy as jnp
from jax import lax
from jax.sharding import PartitionSpec as P


def cut_along(value, dim, count):
    shape = value.shape
    tiles = value.reshape(*shape[:dim], count, shape[dim] // count, *shape[dim + 1 :])
    return jnp.moveaxis(tiles, dim, 0)


def sum_at_owner(value, axis, dim):
    tiles = cut_along(value, dim, lax.axis_size(axis))
    arrived = lax.all_to_all(tiles, axis, split_axis=0, concat_axis=0, tiled=True)
    return arrived.sum(axis=0)


def place_rows(target, slot_count, capacity):
    onehot = (target[:, None] == jnp.arange(slot_count, dtype=jnp.int32)[None, :]).astype(jnp.int32)
    ranks = jnp.sum(jnp.cumsum(onehot, axis=0) * onehot, axis=1) - 1
    return target * capacity + ranks


def local(
    currents, branch_owner, branch_slot, history, coefficients, delays, slab_owner, slab_offset
):
    row_count = lax.axis_size("row")
    col_count = lax.axis_size("col")
    device_count = row_count * col_count
    branch_rows, scenarios = currents.shape
    owned = history.shape[1] // row_count
    capacity = 8 * branch_rows // device_count
    slab_count = slab_owner.shape[0]
    slab_capacity = max(2, 8 * slab_count // device_count)
    owners = jnp.concatenate([branch_owner[:, 0], branch_owner[:, 1]])
    slots = jnp.concatenate([branch_slot[:, 0], branch_slot[:, 1]])
    values = jnp.concatenate([-currents, currents], axis=0)
    target = owners % row_count * col_count + owners // row_count
    position = place_rows(target, device_count, capacity)
    send_values = (
        jnp.zeros((device_count * capacity, scenarios), jnp.float32).at[position].set(values)
    )
    send_slots = jnp.zeros((device_count * capacity,), jnp.int32).at[position].set(slots)
    recv_values, recv_slots = (
        lax.all_to_all(send_values, ("row", "col"), split_axis=0, concat_axis=0, tiled=True),
        lax.all_to_all(send_slots, ("row", "col"), split_axis=0, concat_axis=0, tiled=True),
    )
    increment = jax.ops.segment_sum(recv_values, recv_slots, num_segments=owned)
    my_row = lax.axis_index("row")
    own_past = lax.dynamic_slice_in_dim(history[0], my_row * owned, owned, 0)
    charge_own = (own_past.astype(jnp.float32) + increment).astype(jnp.bfloat16)
    row_blocks, col_blocks = delays.shape
    block_size = coefficients.shape[1] // col_blocks
    past_blocks = history.reshape(history.shape[0], col_blocks, block_size, scenarios)
    column_ids = jnp.arange(col_blocks, dtype=jnp.int32)[None, :]
    earlier = past_blocks[jnp.maximum(delays - 1, 0), column_ids]
    charge_col = lax.all_gather(charge_own, "row", axis=0, tiled=True)
    now_blocks = charge_col.reshape(col_blocks, block_size, scenarios)
    source = jnp.where((delays == 0)[:, :, None, None], now_blocks[None], earlier)
    source = source.reshape(row_blocks, col_blocks * block_size, scenarios)
    coef_rows = coefficients.reshape(row_blocks, block_size, coefficients.shape[1])
    partial_rows = jnp.einsum("rkc,rcs->rks", coef_rows, source, preferred_element_type=jnp.float32)
    partial_rows = partial_rows.reshape(row_blocks * block_size, scenarios)
    asked_owner = jnp.concatenate([slab_owner[:, 0], slab_owner[:, 1]])
    asked_place = jnp.concatenate([slab_offset[:, 0], slab_offset[:, 1]])
    asked_position = place_rows(asked_owner, device_count, slab_capacity)
    request = (
        jnp.zeros((device_count * slab_capacity,), jnp.int32).at[asked_position].set(asked_place)
    )
    incoming = lax.all_to_all(request, ("row", "col"), split_axis=0, concat_axis=0, tiled=True)
    owner_rows = sum_at_owner(partial_rows, "col", 0)
    answers = owner_rows[incoming]
    replies = lax.all_to_all(answers, ("row", "col"), split_axis=0, concat_axis=0, tiled=True)
    picked = replies[asked_position]
    drops = picked[:slab_count] - picked[slab_count:]
    return (charge_col, drops)


def solution(mesh):
    placed = (
        P(("row", "col"), None),
        P(("row", "col"), None),
        P(("row", "col"), None),
        P(None, "col", None),
        P("row", "col"),
        P("row", "col"),
        P(("row", "col"), None),
        P(("row", "col"), None),
    )
    return jax.shard_map(
        local,
        mesh=mesh,
        in_specs=placed,
        out_specs=(P("col", None), P(("row", "col"), None)),
        check_vma=False,
    )
```

profile of v0, /device:TPU:1, one launch (start us, length us, event | category | flops | bytes accessed | tf_op | source)
XLA Modules:
  0.0 178.5 jit_solution(10536520087471744469)
XLA Ops:
  7.2 0.8 fusion.27
  7.9 0.1 copy.13
  8.1 0.2 fusion.6
  8.4 0.2 fusion.5
  8.7 0.8 fusion.26
  9.4 2.5 %scatter_custom_fusion = s32[2048]{0:T(1024)S(1)} fusion(s32[512]{0:T(512)S(1)} %bitcast.74, s32[512]{0:T(512)S(1)} %pad_add_fusion.2, s32[]{:T(128)} %constant.36.clone.1), kind=kCustom, calls=%fused_computation.36 | custom fusion | bytes 8196 | tf_op jit(solution)/shard_map/scatter | solution.py:44
  11.9 0.7 all_to_all.33
  12.6 11.5 %all-to-all-start = ((s32[128,16,1]{1,2,0:T(1,128)}), s32[128,16,1]{1,2,0:T(1,128)S(1)}, u32[]{:S(2)}, u32[]{:S(2)}) async-start(s32[128,16,1]{1,2,0:T(1,128)} %bitcast.11), calls=%async_computation | async-start | bytes 131072 | tf_op jit(solution)/shard_map/all_to_all | solution.py:47
  24.1 1.0 neg.3
  25.1 4.1 %scatter_custom_fusion.1 = f32[2048,256]{1,0:T(8,128)} fusion(s32[512]{0:T(512)S(1)} %bitcast.75, f32[]{:T(128)} %constant.73.clone.1, f32[256,256]{1,0:T(8,128)} %param.8, f32[]{:T(128)} %constant.100, f32[256,256]{1,0:T(8,128)S(1)} %neg.3), kind=kCustom, calls=%fused_computation.8 | custom fusion | flops 131072 | bytes 2621448 | tf_op jit(solution)/shard_map/scatter | solution.py:42
  29.2 4.4 %all-to-all-done = s32[128,16,1]{1,2,0:T(1,128)S(1)} async-done(((s32[128,16,1]{1,2,0:T(1,128)}), s32[128,16,1]{1,2,0:T(1,128)S(1)}, u32[]{:S(2)}, u32[]{:S(2)}) %all-to-all-start) | async-done | bytes 8224 | tf_op jit(solution)/shard_map/all_to_all | solution.py:47
  33.6 5.3 %all-to-all-start.1 = ((f32[128,16,256]{2,1,0:T(8,128)}), f32[128,16,256]{2,1,0:T(8,128)S(1)}, u32[]{:S(2)}, u32[]{:S(2)}) async-start(f32[128,16,256]{2,1,0:T(8,128)} %bitcast.62), calls=%async_computation.1 | async-start | bytes 4194304 | tf_op jit(solution)/shard_map/all_to_all | solution.py:46
  39.0 0.0 all-gather.2.cloned.1.call-start
  39.0 4.5 %slice.39 = bf16[1,8192,256]{2,1,0:T(8,128)(2,1)} slice(bf16[4,8192,256]{2,1,0:T(8,128)(2,1)} %param.11), slice={[0:1], [0:8192], [0:256]} | slice | bytes 8388608 | tf_op jit(solution)/shard_map/slice | solution.py:51
  43.5 1.1 bitcast_convert_fusion
  44.6 0.5 broadcast.346
  45.2 0.8 reduce.6
  45.9 0.1 reshape.422
  46.0 22.3 %all-to-all-done.1 = f32[128,16,256]{2,1,0:T(8,128)S(1)} async-done(((f32[128,16,256]{2,1,0:T(8,128)}), f32[128,16,256]{2,1,0:T(8,128)S(1)}, u32[]{:S(2)}, u32[]{:S(2)}) %all-to-all-start.1) | async-done | bytes 2097184 | tf_op jit(solution)/shard_map/all_to_all | solution.py:46
  68.3 0.0 copy-start
  68.3 0.0 copy-start.1
  68.3 0.0 copy-start.2
  68.3 13.4 %scatter_fusion = f32[1024,256]{1,0:T(8,128)S(1)} fusion(f32[1024,256]{1,0:T(8,128)S(1)} %bitcast_convert_fusion, s32[2048]{0:T(1024)S(1)} %reshape.422, f32[2048,256]{1,0:T(8,128)S(1)} %bitcast.61), kind=kCustom, calls=%fused_computation.5 | custom fusion | flops 524288 | bytes 6299648 | tf_op jit(solution)/shard_map/scatter-add | solution.py:49
  81.8 0.8 convert_element_type.20
  82.6 0.0 all-gather.2.cloned.1.call-update
  82.6 0.0 copy-done
  82.7 0.1 pad_add_fusion.3
  82.7 0.1 fusion.9
  82.8 0.2 reduce_window_sum.28
  83.0 0.0 copy-done.1
  83.0 0.1 pad_add_fusion.4
  83.1 0.2 select_reduce_fusion
  83.3 0.1 fusion.24
  83.3 1.0 scatter_custom_fusion.3
  84.3 0.7 all_to_all.39
  85.1 4.9 %all-to-all-start.3 = ((s32[128,4,1]{1,2,0:T(1,128)}), s32[128,4,1]{1,2,0:T(1,128)S(1)}, u32[]{:S(2)}, u32[]{:S(2)}) async-start(s32[128,4,1]{1,2,0:T(1,128)} %bitcast.26), calls=%async_computation.3 | async-start | bytes 131072 | tf_op jit(solution)/shard_map/all_to_all | solution.py:71
  90.0 0.0 copy-done.2
  90.1 0.1 reshape.382
  90.1 0.1 broadcast_bitcast_fusion
  90.3 11.7 %gather_fusion = bf16[64,256,256]{2,1,0:T(8,128)(2,1)} fusion(bf16[4,32,256,256]{3,2,1,0:T(8,128)(2,1)} %bitcast.60, s32[64]{0:T(128)S(1)} %reshape.382), kind=kCustom, calls=%fused_computation | custom fusion | bytes 16777728 | tf_op jit(solution)/shard_map/gather | solution.py:57
  101.9 10.6 %all-gather.2.cloned.1.call-done = bf16[8192,256]{1,0:T(8,128)(2,1)} async-done(((bf16[1024,256]{1,0:T(8,128)(2,1)}), bf16[8192,256]{1,0:T(8,128)(2,1)}) %all-gather.2.cloned.1.call-update) | async-done | bytes 4194320 | tf_op jit(solution)/shard_map/all_gather | solution.py:58
  112.5 7.0 %bitcast_select_fusion = bf16[2,8192,256]{2,1,0:T(8,128)(2,1)S(1)} fusion(pred[2,8192]{1,0:T(4,128)(4,1)S(1)} %bitcast.65, bf16[8192,256]{1,0:T(8,128)(2,1)} %all-gather.2.cloned.1.call-done, bf16[2,8192,256]{2,1,0:T(8,128)(2,1)} %bitcast.59), kind=kLoop, calls=%fused_computation.7 | loop fusion | flops 4194304 | bytes 20987904 | tf_op jit(solution)/shard_map/jit(_where)/select_n | solution.py:60
  119.5 6.5 %fusion.29 = f32[2,256,256]{1,2,0:T(8,128)} fusion(bf16[2,256,8192]{2,1,0:T(8,128)(2,1)} %bitcast.76, bf16[2,8192,256]{2,1,0:T(8,128)(2,1)S(1)} %bitcast_select_fusion), kind=kOutput, calls=%fused_computation.82 | convolution fusion | flops 2147483648 | bytes 17301504 | tf_op jit(solution)/shard_map/rkc,rcs->rks/dot_general | solution.py:63
  126.0 0.0 all-to-all-done.3
  126.0 6.8 %all-to-all-start.2 = ((f32[16,32,256]{2,1,0:T(8,128)}), f32[16,32,256]{2,1,0:T(8,128)S(1)}, u32[]{:S(2)}, u32[]{:S(2)}) async-start(f32[16,32,256]{2,1,0:T(8,128)} %bitcast.19), calls=%async_computation.2 | async-start | bytes 1048576 | tf_op jit(solution)/shard_map/all_to_all | solution.py:15
  132.8 0.8 reduce.7
  133.5 0.1 all_to_all.41
  133.7 9.4 %all-to-all-done.2 = f32[16,32,256]{2,1,0:T(8,128)S(1)} async-done(((f32[16,32,256]{2,1,0:T(8,128)}), f32[16,32,256]{2,1,0:T(8,128)S(1)}, u32[]{:S(2)}, u32[]{:S(2)}) %all-to-all-start.2) | async-done | bytes 524320 | tf_op jit(solution)/shard_map/all_to_all | solution.py:15
  143.1 1.6 gather_fusion.1
  144.7 0.9 all_to_all.42
  145.7 6.1 %all-to-all-start.4 = ((f32[128,4,256]{2,1,0:T(4,128)}), f32[128,4,256]{2,1,0:T(4,128)S(1)}, u32[]{:S(2)}, u32[]{:S(2)}) async-start(f32[128,4,256]{2,1,0:T(4,128)} %all_to_all.42), calls=%async_computation.4 | async-start | bytes 1048576 | tf_op jit(solution)/shard_map/all_to_all | solution.py:74
  151.8 13.8 %all-to-all-done.4 = f32[128,4,256]{2,1,0:T(4,128)S(1)} async-done(((f32[128,4,256]{2,1,0:T(4,128)}), f32[128,4,256]{2,1,0:T(4,128)S(1)}, u32[]{:S(2)}, u32[]{:S(2)}) %all-to-all-start.4) | async-done | bytes 524320 | tf_op jit(solution)/shard_map/all_to_all | solution.py:74
  165.6 0.2 all_to_all.44
  165.8 0.8 gather_fusion.2
  166.5 0.6 slice_subtract_fusion
  167.2 4.5 %copy.20 = bf16[8192,256]{1,0:T(8,128)(2,1)} copy(bf16[8192,256]{1,0:T(8,128)(2,1)} %all-gather.2.cloned.1.call-done) | data formatting | bytes 8388608
  (21 shorter events, 0.3 us)
Async XLA Ops:
  12.6 21.0 %all-to-all-start = ((s32[128,16,1]{1,2,0:T(1,128)}), s32[128,16,1]{1,2,0:T(1,128)S(1)}, u32[]{:S(2)}, u32[]{:S(2)}) async-start(s32[128,16,1]{1,2,0:T(1,128)} %bitcast.11), calls=%async_computation | async-start | bytes 131072 | tf_op jit(solution)/shard_map/all_to_all | solution.py:47
  33.6 34.7 %all-to-all-start.1 = ((f32[128,16,256]{2,1,0:T(8,128)}), f32[128,16,256]{2,1,0:T(8,128)S(1)}, u32[]{:S(2)}, u32[]{:S(2)}) async-start(f32[128,16,256]{2,1,0:T(8,128)} %bitcast.62), calls=%async_computation.1 | async-start | bytes 4194304 | tf_op jit(solution)/shard_map/all_to_all | solution.py:46
  39.0 73.5 %all-gather.2.cloned.1.call-start = ((), (), s32[]{:S(2)}) async-start(), calls=%async_computation.5 | async-start | bytes 4718592 | tf_op jit(solution)/shard_map/all_gather | solution.py:58
  68.3 14.3 %copy-start = (s32[64,2]{0,1:T(2,128)S(1)}, s32[64,2]{0,1:T(2,128)}, u32[]{:S(2)}) copy-start(s32[64,2]{0,1:T(2,128)} %param.14) | copy-start | bytes 1540
  68.3 14.7 %copy-start.1 = (s32[64,2]{0,1:T(2,128)S(1)}, s32[64,2]{0,1:T(2,128)}, u32[]{:S(2)}) copy-start(s32[64,2]{0,1:T(2,128)} %param.15) | copy-start | bytes 1540
  68.3 21.7 %copy-start.2 = (s32[2,32]{1,0:T(2,128)S(1)}, s32[2,32]{1,0:T(2,128)}, u32[]{:S(2)}) copy-start(s32[2,32]{1,0:T(2,128)} %param.13) | copy-start | bytes 772
  85.1 40.9 %all-to-all-start.3 = ((s32[128,4,1]{1,2,0:T(1,128)}), s32[128,4,1]{1,2,0:T(1,128)S(1)}, u32[]{:S(2)}, u32[]{:S(2)}) async-start(s32[128,4,1]{1,2,0:T(1,128)} %bitcast.26), calls=%async_computation.3 | async-start | bytes 131072 | tf_op jit(solution)/shard_map/all_to_all | solution.py:71
  126.0 17.1 %all-to-all-start.2 = ((f32[16,32,256]{2,1,0:T(8,128)}), f32[16,32,256]{2,1,0:T(8,128)S(1)}, u32[]{:S(2)}, u32[]{:S(2)}) async-start(f32[16,32,256]{2,1,0:T(8,128)} %bitcast.19), calls=%async_computation.2 | async-start | bytes 1048576 | tf_op jit(solution)/shard_map/all_to_all | solution.py:15
  145.7 19.9 %all-to-all-start.4 = ((f32[128,4,256]{2,1,0:T(4,128)}), f32[128,4,256]{2,1,0:T(4,128)S(1)}, u32[]{:S(2)}, u32[]{:S(2)}) async-start(f32[128,4,256]{2,1,0:T(4,128)} %all_to_all.42), calls=%async_computation.4 | async-start | bytes 1048576 | tf_op jit(solution)/shard_map/all_to_all | solution.py:74
Sparse Core Ops, SparseCore 0:
  82.8 29.6 all-gather.1
where the time goes:
time: 179 us; the launch traced here: 178 us
  waiting for transfers between devices  60.6 us (34%)
  starting transfers between devices  34.6 us (19%)
  local copies, waits for them, and re-layouts  31.6 us (18%)
  other arithmetic  30.9 us (17%)
  between operations  14.3 us (8%)
  matrix products  6.5 us (4%)
    all_to_all x1, waiting for transfers between devices, local(): lax.all_to_all(send_values, ('row', 'col'), split_axis=0, concat_axis=0,...  22.3 us
    all_to_all x1, waiting for transfers between devices, local(): lax.all_to_all(answers, ('row', 'col'), split_axis=0, concat_axis=0, tile...  13.8 us
    scatter-add x1, other arithmetic, local(): increment = jax.ops.segment_sum(recv_values, recv_slots, num_segments=owned)  13.4 us
    gather x1, local copies, waits for them, and re-layouts, local(): earlier = past_blocks[jnp.maximum(delays - 1, 0), column_ids]  11.7 us
    all_to_all x1, starting transfers between devices, local(): lax.all_to_all(send_slots, ('row', 'col'), split_axis=0, concat_axis=0, t...  11.5 us
    all_gather x1, waiting for transfers between devices, local(): charge_col = lax.all_gather(charge_own, 'row', axis=0, tiled=True)  10.6 us
    all_to_all x1, waiting for transfers between devices, sum_at_owner(): lax.all_to_all(tiles, axis, split_axis=0, concat_axis=0, tiled=True)  9.43 us
    select_n x1, other arithmetic, local(): jnp.where((delays == 0)[:, :, None, None], now_blocks[None], earlier)  6.99 us
  transfers between devices with their start and end apart: 6, of which 5 were waited for; matrix products, arithmetic and copies ran while one was open for 22% of the time, Pallas kernels for 0%

commit v1 on v0

v1 whole, which is shorter than its diff:
```python
import functools

import jax
import jax.numpy as jnp
from jax import lax
from jax.experimental import pallas as pl
from jax.experimental.pallas import tpu as pltpu
from jax.sharding import PartitionSpec as P

F32 = jnp.float32
BF16 = jnp.bfloat16
I32 = jnp.int32
MESH = pl.DeviceIdType.MESH

ROWS = 8
COLS = 16
DEV = ROWS * COLS
CORES = 2
XS = ROWS // CORES
BRANCH = 256
CAP = 16
SCAP = 4
OWN = 1024
EXC = 256
HALF = 128
SLOTS = DEV * CAP
BLK = 256
PIECES = 4
PIECE = OWN // PIECES


def iota(shape, dim):
    return lax.broadcasted_iota(I32, shape, dim)


def nn(a, b):
    return lax.dot_general(a, b, (((1,), (0,)), ((), ())), preferred_element_type=F32)


def nt(a, b):
    return lax.dot_general(a, b, (((1,), (1,)), ((), ())), preferred_element_type=F32)


def tn(a, b):
    return lax.dot_general(a, b, (((0,), (0,)), ((), ())), preferred_element_type=F32)


def device_of(index):
    return (index // COLS, lax.rem(index, COLS))


def ranks_of(first, second):
    n = first.shape[1]
    hot_a = iota((DEV, n), 0) == first
    hot_b = iota((DEV, n), 0) == second
    a, b = hot_a.astype(F32), hot_b.astype(F32)
    before = (iota((n, n), 0) < iota((n, n), 1)).astype(BF16)
    seen_a = nn(a.astype(BF16), before)
    seen_b = nn(b.astype(BF16), before) + jnp.sum(a, axis=1, keepdims=True)
    rank_a = jnp.sum(a * seen_a, axis=0, keepdims=True).astype(I32)
    rank_b = jnp.sum(b * seen_b, axis=0, keepdims=True).astype(I32)
    return a.astype(BF16), b.astype(BF16), rank_a, rank_b


def greet(me):
    barrier = pltpu.get_barrier_semaphore()

    def signal(t, _):
        other = lax.rem(me + t, DEV)
        pl.semaphore_signal(barrier, inc=1, device_id=device_of(other), device_id_type=MESH)
        return 0

    lax.fori_loop(1, DEV, signal, 0)
    return barrier


def exchange_kernel(
    delays, cur, owner, slot, sowner, soffset, hist, coef,
    charge_out, acc, meta_in,
    send, recv, meta_out, planes, q_hi, q_lo, past, gathered,
    hist_a, hist_b, coef_a, coef_b,
    v_send, v_recv, m_send, m_recv, self_sem, past_sem, in_sem, out_sem,
    g_send, g_near, g_pair,
):
    row, col = lax.axis_index("row"), lax.axis_index("col")
    me = row * COLS + col
    barrier = greet(me)
    past_copy = pltpu.make_async_copy(hist.at[0, pl.ds(pl.multiple_of(row * OWN, OWN), OWN)], past, past_sem)
    past_copy.start()

    width = 2 * BLK
    steps = coef.shape[1] // width
    buffers = ((hist_a, coef_a), (hist_b, coef_b))

    def stream(step, which):
        at = pl.ds(pl.multiple_of(step * width, width), width)
        h, c = buffers[which]
        return (
            pltpu.make_async_copy(hist.at[:, at], h, in_sem.at[which, 0]),
            pltpu.make_async_copy(coef.at[:, at], c, in_sem.at[which, 1]),
        )

    for which in range(2):
        for copy in stream(which, which):
            copy.start()

    own = owner[...]
    targets = (own & (ROWS - 1)) * COLS + (own >> 3)
    t_from, t_to = targets[0:1, :], targets[1:2, :]
    hot_from, hot_to, r_from, r_to = ranks_of(t_from, t_to)
    p_from, p_to = t_from * CAP + r_from, t_to * CAP + r_to
    x = cur[...]
    size = jnp.abs(x)
    size = jnp.maximum(size[:, :HALF], size[:, HALF:])
    largest = jnp.max(size.T, axis=0, keepdims=True)
    scale = jnp.full((1, BRANCH), 2.0**-12, F32)
    inverse = jnp.full((1, BRANCH), 2.0**12, F32)
    for _ in range(32):
        smaller = largest <= scale * 16383.0
        scale = jnp.where(smaller, scale * 0.5, scale)
        inverse = jnp.where(smaller, inverse * 2.0, inverse)
    spread = jnp.broadcast_to(inverse, (HALF, BRANCH)).T
    q = jnp.round(x * jnp.concatenate([spread, spread], axis=1))
    high = jnp.floor(q * (1.0 / 256.0))
    q_hi[...] = high.astype(BF16)
    q_lo[...] = (q - high * 256.0).astype(BF16)

    def told(rank, number):
        line = iota((HALF, BRANCH), 0)
        s = number.astype(I32)
        words = jnp.where(line == rank, (s >> 5).astype(F32), 0.0)
        words = words + jnp.where(line == rank + 16, (s & 31).astype(F32), 0.0)
        return (words + jnp.where(line == rank + 32, scale, 0.0)).astype(BF16)

    s_own, s_off = sowner[...], soffset[...]
    hot_0, hot_1, s_0, s_1 = ranks_of(s_own[0:1, :], s_own[1:2, :])

    def asked(rank, offset):
        line = iota((HALF, offset.shape[1]), 0)
        return jnp.where(line == rank + 48, offset.astype(F32), 0.0).astype(BF16)

    slots = slot[...]
    words = nt(hot_from, told(r_from, slots[0:1, :])) + nt(hot_to, told(r_to, slots[1:2, :]))
    words = words + nt(hot_0, asked(s_0, s_off[0:1, :])) + nt(hot_1, asked(s_1, s_off[1:2, :]))
    meta_out[...] = words.reshape(DEV, 1, HALF)

    chunk = 256

    def fill(t, _):
        place = iota((chunk, BRANCH), 0) + t * chunk
        sign = (place == p_to).astype(F32) - (place == p_from).astype(F32)
        sign = sign.astype(BF16)
        value = (nn(sign, q_hi[...]) * 256.0 + nn(sign, q_lo[...])).astype(I32)
        word = (value[:, :HALF] << 16) | (value[:, HALF:] & 0xFFFF)
        send[pl.ds(pl.multiple_of(t * chunk, chunk), chunk), :] = word
        return 0

    lax.fori_loop(0, SLOTS // chunk, fill, 0)

    pl.semaphore_wait(barrier, DEV - 1)

    def chunk_of(index):
        return pl.ds(pl.multiple_of(index * CAP, CAP), CAP)

    def out(t, _):
        other = lax.rem(me + t, DEV)
        pltpu.make_async_remote_copy(
            meta_out.at[other], meta_in.at[me], m_send, m_recv,
            device_id=device_of(other), device_id_type=MESH,
        ).start()
        pltpu.make_async_remote_copy(
            send.at[chunk_of(other)], recv.at[chunk_of(me)], v_send, v_recv,
            device_id=device_of(other), device_id_type=MESH,
        ).start()
        return 0

    lax.fori_loop(1, DEV, out, 0)
    self_v = pltpu.make_async_copy(send.at[chunk_of(me)], recv.at[chunk_of(me)], self_sem.at[0])
    self_m = pltpu.make_async_copy(meta_out.at[me], meta_in.at[me], self_sem.at[1])
    self_v.start()
    self_m.start()

    acc[...] = jnp.zeros_like(acc)

    def delayed(pair, _):
        for which in range(2):
            step = pair * 2 + which
            for copy in stream(step, which):
                copy.wait()
            h, c = buffers[which]
            for i in range(2):
                total = acc[pl.ds(i * BLK, BLK), :]
                for k in range(2):
                    d = delays[i, step * 2 + k]
                    source = h[jnp.maximum(d - 1, 0), pl.ds(k * BLK, BLK), :]
                    part = nn(c[pl.ds(i * BLK, BLK), pl.ds(k * BLK, BLK)], source)
                    total = total + jnp.where(d > 0, part, 0.0)
                acc[pl.ds(i * BLK, BLK), :] = total

            @pl.when(pair < steps // 2 - 1)
            def _():
                for copy in stream(step + 2, which):
                    copy.start()

        return 0

    lax.fori_loop(0, steps // 2, delayed, 0)

    self_v.wait()
    self_m.wait()
    rest = pl.ds(0, DEV - 1)
    pltpu.make_async_copy(meta_in.at[rest], meta_in.at[rest], m_recv).wait()
    rest = pl.ds(0, (DEV - 1) * CAP)
    pltpu.make_async_copy(recv.at[rest], recv.at[rest], v_recv).wait()

    heard = meta_in[...].reshape(DEV, HALF).astype(BF16)
    expand = ((iota((DEV, SLOTS), 1) >> 4) == iota((DEV, SLOTS), 0)).astype(BF16)
    wide = tn(heard, expand)
    line = iota((16, SLOTS), 0)
    mine = line == (iota((16, SLOTS), 1) & 15)

    def picked(first):
        return jnp.sum(jnp.where(mine, wide[first : first + 16, :], 0.0), axis=0, keepdims=True)

    node = (picked(0) * 32.0 + picked(16)).astype(I32)
    weight = picked(32)

    def unpack(t, _):
        at = pl.ds(pl.multiple_of(t * chunk, chunk), chunk)
        w = recv[at, :]
        planes[at, 0 * HALF : 1 * HALF] = (w >> 24).astype(F32).astype(BF16)
        planes[at, 1 * HALF : 2 * HALF] = ((w << 16) >> 24).astype(F32).astype(BF16)
        planes[at, 2 * HALF : 3 * HALF] = ((w >> 16) & 255).astype(F32).astype(BF16)
        planes[at, 3 * HALF : 4 * HALF] = (w & 255).astype(F32).astype(BF16)
        return 0

    lax.fori_loop(0, SLOTS // chunk, unpack, 0)
    past_copy.wait()

    xpos, core = row // CORES, lax.rem(row, CORES)
    right, left, far = lax.rem(xpos + 1, XS), lax.rem(xpos + XS - 1, XS), lax.rem(xpos + 2, XS)

    def piece(at_x, at_core, j):
        start = (at_x * CORES + at_core) * OWN + j * PIECE
        return pl.ds(pl.multiple_of(start, PIECE), PIECE)

    def move(at_x, at_core, j, to_x, to_core, sem, recv_sem):
        at = piece(at_x, at_core, j)
        return pltpu.make_async_remote_copy(
            gathered.at[at], gathered.at[at], sem, recv_sem,
            device_id=(to_x * CORES + to_core, col), device_id_type=MESH,
        )

    sent, written = [], []

    def begin(copy):
        copy.start()
        sent.append(copy)

    def write(at_x, at_core, j, sem):
        at = piece(at_x, at_core, j)
        copy = pltpu.make_async_copy(gathered.at[at], charge_out.at[at], sem)
        copy.start()
        written.append(copy)

    order = (0, 2, 1, 3)
    other = 1 - core
    for j in order:
        spot = iota((PIECE, SLOTS), 0) + j * PIECE
        gate = jnp.where(spot == node, weight, 0.0).astype(BF16)
        both = nn(gate, planes[...])
        rise = both[:, :EXC] * 256.0 + both[:, EXC:]
        fresh = past[pl.ds(j * PIECE, PIECE), :].astype(F32) + rise
        gathered[piece(xpos, core, j), :] = fresh.astype(BF16)
        a = (right, left) if j < 2 else (left, right)
        for n, to in enumerate(a):
            side = 0 if to is right else 1
            begin(move(xpos, core, j, to, core, g_send.at[side, j], g_near.at[side, j]))
        begin(move(xpos, core, j, xpos, other, g_send.at[2, j], g_pair.at[0, j]))
        write(xpos, core, j, out_sem.at[0, j])

    def arrived(at_x, at_core, j, recv_sem):
        at = piece(at_x, at_core, j)
        pltpu.make_async_copy(gathered.at[at], gathered.at[at], recv_sem).wait()

    for j in order:
        arrived(left, core, j, g_near.at[0, j])
        if j < 2:
            begin(move(left, core, j, right, core, g_send.at[3, j], g_near.at[2, j]))
        begin(move(left, core, j, xpos, other, g_send.at[4, j], g_pair.at[1, j]))
        write(left, core, j, out_sem.at[1, j])
        arrived(right, core, j, g_near.at[1, j])
        if j >= 2:
            begin(move(right, core, j, left, core, g_send.at[3, j], g_near.at[2, j]))
        begin(move(right, core, j, xpos, other, g_send.at[5, j], g_pair.at[2, j]))
        write(right, core, j, out_sem.at[2, j])
    for j in order:
        arrived(far, core, j, g_near.at[2, j])
        begin(move(far, core, j, xpos, other, g_send.at[6, j], g_pair.at[3, j]))
        write(far, core, j, out_sem.at[3, j])
    for n, at_x in enumerate((xpos, left, right, far)):
        for j in order:
            arrived(at_x, other, j, g_pair.at[n, j])
            write(at_x, other, j, out_sem.at[4 + n, j])
    for copy in sent:
        copy.wait_send()
    for copy in written:
        copy.wait()
    rest = pl.ds(0, DEV - 1)
    pltpu.make_async_copy(meta_out.at[rest], meta_out.at[rest], m_send).wait()
    rest = pl.ds(0, (DEV - 1) * CAP)
    pltpu.make_async_copy(send.at[rest], send.at[rest], v_send).wait()


def exchange(delays, cur, owner, slot, sowner, soffset, hist, coef):
    vmem, hbm = pl.BlockSpec(memory_space=pltpu.VMEM), pl.BlockSpec(memory_space=pl.ANY)
    nodes = hist.shape[1]
    width = 2 * BLK
    dma = pltpu.SemaphoreType.DMA
    return pl.pallas_call(
        exchange_kernel,
        out_shape=(
            jax.ShapeDtypeStruct((nodes, EXC), BF16),
            jax.ShapeDtypeStruct((coef.shape[0], EXC), F32),
            jax.ShapeDtypeStruct((DEV, 1, HALF), F32),
        ),
        in_specs=[pl.BlockSpec(memory_space=pltpu.SMEM)] + [vmem] * 5 + [hbm] * 2,
        out_specs=(hbm, vmem, vmem),
        scratch_shapes=[
            pltpu.VMEM((SLOTS, HALF), I32),
            pltpu.VMEM((SLOTS, HALF), I32),
            pltpu.VMEM((DEV, 1, HALF), F32),
            pltpu.VMEM((SLOTS, 2 * EXC), BF16),
            pltpu.VMEM((BRANCH, EXC), BF16),
            pltpu.VMEM((BRANCH, EXC), BF16),
            pltpu.VMEM((OWN, EXC), BF16),
            pltpu.VMEM((nodes, EXC), BF16),
            pltpu.VMEM((4, width, EXC), BF16),
            pltpu.VMEM((4, width, EXC), BF16),
            pltpu.VMEM((coef.shape[0], width), BF16),
            pltpu.VMEM((coef.shape[0], width), BF16),
            dma, dma, dma, dma, dma((2,)), dma, dma((2, 2)), dma((8, PIECES)),
            dma((7, PIECES)), dma((3, PIECES)), dma((4, PIECES)),
        ],
        compiler_params=pltpu.CompilerParams(
            collective_id=0, has_side_effects=True, vmem_limit_bytes=48 << 20
        ),
        name="exchange",
    )(delays, cur, owner, slot, sowner, soffset, hist, coef)


def current_kernel(delays, acc, charge, coef, total, charge_now, block, weights, in_sem, out_sem, c_sem):
    span = 4 * BLK
    parts = charge.shape[0] // span

    def coefficient(i, k):
        at = pl.ds(pl.multiple_of(k * BLK, BLK), BLK)
        return pltpu.make_async_copy(
            coef.at[pl.ds(i * BLK, BLK), at], weights.at[i, k], c_sem.at[i, k]
        )

    def load(part):
        at = pl.ds(pl.multiple_of(part * span, span), span)
        return pltpu.make_async_copy(charge.at[at], block.at[at], in_sem.at[part])

    def save(part):
        at = pl.ds(pl.multiple_of(part * span, span), span)
        return pltpu.make_async_copy(block.at[at], charge_now.at[at], out_sem.at[part])

    for part in range(parts):
        load(part).start()

    def ask(k, _):
        for i in range(2):
            @pl.when(delays[i, k] == 0)
            def _():
                coefficient(i, k).start()

        return 0

    lax.fori_loop(0, parts * 4, ask, 0)
    total[...] = acc[...]
    for part in range(parts):
        load(part).wait()
        save(part).start()

        def work(n, _):
            k = part * 4 + n
            for i in range(2):
                @pl.when(delays[i, k] == 0)
                def _():
                    coefficient(i, k).wait()
                    source = block[pl.ds(pl.multiple_of(k * BLK, BLK), BLK), :]
                    total[pl.ds(i * BLK, BLK), :] += nn(weights[i, k], source)

            return 0

        lax.fori_loop(0, 4, work, 0)
    for part in range(parts):
        save(part).wait()


def current(delays, acc, charge, coef):
    vmem, hbm = pl.BlockSpec(memory_space=pltpu.VMEM), pl.BlockSpec(memory_space=pl.ANY)
    dma = pltpu.SemaphoreType.DMA
    blocks = charge.shape[0] // BLK
    return pl.pallas_call(
        current_kernel,
        out_shape=(
            jax.ShapeDtypeStruct(acc.shape, F32),
            jax.ShapeDtypeStruct(charge.shape, BF16),
        ),
        in_specs=[pl.BlockSpec(memory_space=pltpu.SMEM), vmem, hbm, hbm],
        out_specs=(vmem, hbm),
        scratch_shapes=[
            pltpu.VMEM(charge.shape, BF16),
            pltpu.VMEM((2, blocks, BLK, BLK), BF16),
            dma((blocks // 4,)), dma((blocks // 4,)), dma((2, blocks)),
        ],
        compiler_params=pltpu.CompilerParams(vmem_limit_bytes=40 << 20),
        name="current",
    )(delays, acc, charge, coef)


def split(value):
    top = value.astype(BF16)
    return top, (value - top.astype(F32)).astype(BF16)


def drops_kernel(
    part, meta, sowner, drops, parts, answer, replies,
    p_send, p_recv, a_send, a_recv, self_sem,
):
    row, col = lax.axis_index("row"), lax.axis_index("col")
    me = row * COLS + col
    barrier = greet(me)
    share = part.shape[0] // COLS
    span = 2 * SCAP
    asked = DEV * span

    heard = meta[...].reshape(DEV, HALF).astype(BF16)
    expand = ((iota((DEV, asked), 1) >> 3) == iota((DEV, asked), 0)).astype(BF16)
    wide = tn(heard, expand)[48:56, :]
    mine = iota((span, asked), 0) == (iota((span, asked), 1) & (SCAP - 1))
    place = jnp.sum(jnp.where(mine, wide, 0.0), axis=0, keepdims=True).astype(I32)
    place = place + share * ((iota((1, asked), 1) >> 2) & 1)
    take = (iota((2 * share, asked), 0) == place).astype(BF16)

    pl.semaphore_wait(barrier, DEV - 1)

    def rows_of(index):
        return pl.ds(pl.multiple_of(index * share, share), share)

    def send_part(t, _):
        other = lax.rem(col + t, COLS)
        pltpu.make_async_remote_copy(
            part.at[rows_of(other)], parts.at[rows_of(col)], p_send, p_recv,
            device_id=(row, other), device_id_type=MESH,
        ).start()
        return 0

    lax.fori_loop(1, COLS, send_part, 0)
    self_p = pltpu.make_async_copy(part.at[rows_of(col)], parts.at[rows_of(col)], self_sem.at[0])
    self_p.start()

    s_own = sowner[...]
    first, second = s_own[0:1, :], s_own[1:2, :]
    _, _, r_0, r_1 = ranks_of(first, second)
    at_0, at_1 = first * span + r_0, second * span + r_1

    self_p.wait()
    rest = pl.ds(0, (COLS - 1) * share)
    pltpu.make_async_copy(parts.at[rest], parts.at[rest], p_recv).wait()
    total = parts[pl.ds(0, share), :]
    for n in range(1, COLS):
        total = total + parts[pl.ds(n * share, share), :]
    stacked = jnp.concatenate([total[:, :HALF], total[:, HALF:]], axis=0)
    top, low = split(stacked)
    answer[...] = tn(take, top) + tn(take, low)

    def chunk_of(index):
        return pl.ds(pl.multiple_of(index * span, span), span)

    def send_answer(t, _):
        other = lax.rem(me + t, DEV)
        pltpu.make_async_remote_copy(
            answer.at[chunk_of(other)], replies.at[chunk_of(me)], a_send, a_recv,
            device_id=device_of(other), device_id_type=MESH,
        ).start()
        return 0

    lax.fori_loop(1, DEV, send_answer, 0)
    self_a = pltpu.make_async_copy(answer.at[chunk_of(me)], replies.at[chunk_of(me)], self_sem.at[1])
    self_a.start()
    self_a.wait()
    rest = pl.ds(0, (DEV - 1) * span)
    pltpu.make_async_copy(replies.at[rest], replies.at[rest], a_recv).wait()
    top, low = split(replies[...])
    both = jnp.concatenate([top, low], axis=1)
    count = first.shape[1]
    line = iota((asked, count), 0)
    for half in range(2):
        shift = half * SCAP
        gate = (line == at_0 + shift).astype(F32) - (line == at_1 + shift).astype(F32)
        found = tn(gate.astype(BF16), both)
        drops[:, half * HALF : (half + 1) * HALF] = found[:, :HALF] + found[:, HALF:]
    pltpu.make_async_copy(answer.at[rest], answer.at[rest], a_send).wait()
    rest = pl.ds(0, (COLS - 1) * share)
    pltpu.make_async_copy(part.at[rest], part.at[rest], p_send).wait()


def find_drops(part, meta, sowner):
    vmem = pl.BlockSpec(memory_space=pltpu.VMEM)
    dma = pltpu.SemaphoreType.DMA
    asked = DEV * 2 * SCAP
    return pl.pallas_call(
        drops_kernel,
        out_shape=jax.ShapeDtypeStruct((sowner.shape[1], EXC), F32),
        in_specs=[vmem] * 3,
        out_specs=vmem,
        scratch_shapes=[
            pltpu.VMEM(part.shape, F32),
            pltpu.VMEM((asked, HALF), F32),
            pltpu.VMEM((asked, HALF), F32),
            dma, dma, dma, dma, dma((2,)),
        ],
        compiler_params=pltpu.CompilerParams(
            collective_id=1, has_side_effects=True, vmem_limit_bytes=24 << 20
        ),
        name="find_drops",
    )(part, meta, sowner)


def local(
    currents, branch_owner, branch_slot, history, coefficients, delays, slab_owner, slab_offset
):
    sowner = slab_owner.T
    charge, acc, meta = exchange(
        delays, currents, branch_owner.T, branch_slot.T, sowner, slab_offset.T, history, coefficients
    )
    part, charge_now = current(delays, acc, charge, coefficients)
    return charge_now, find_drops(part, meta, sowner)


def solution(mesh):
    placed = (
        P(("row", "col"), None),
        P(("row", "col"), None),
        P(("row", "col"), None),
        P(None, "col", None),
        P("row", "col"),
        P("row", "col"),
        P(("row", "col"), None),
        P(("row", "col"), None),
    )
    return jax.shard_map(
        local,
        mesh=mesh,
        in_specs=placed,
        out_specs=(P("col", None), P(("row", "col"), None)),
        check_vma=False,
    )
```

time: 179 us -> 96.9 us (0.54)
  Pallas kernels: 0 us -> 86.7 us
  waiting for transfers between devices: 60.6 us -> 0 us
  starting transfers between devices: 34.6 us -> 0 us
  other arithmetic: 30.9 us -> 0 us
  local copies, waits for them, and re-layouts: 31.6 us -> 9.17 us
  between operations: 14.3 us -> 0.68 us
  matrix products: 6.5 us -> 0 us
    pallas_call x0 -> x3, Pallas kernels: none -> 86.7 us  [the longest x1 51.1 us: exchange(): pl.pallas_call(exchange_kernel, out_shape=(jax.ShapeDtypeStruct((nodes, E...]
    all_to_all x5 -> x0, waiting for transfers between devices: 50 us -> none  [the longest x1 22.3 us: local(): lax.all_to_all(send_values, ('row', 'col'), split_axis=0, concat_axis=0,...]
    all_to_all x5 -> x0, starting transfers between devices: 34.6 us -> none  [the longest x1 11.5 us: local(): lax.all_to_all(send_slots, ('row', 'col'), split_axis=0, concat_axis=0, t...]
    gather x3 -> x0, local copies, waits for them, and re-layouts: 14 us -> none  [the longest x1 11.7 us: local(): earlier = past_blocks[jnp.maximum(delays - 1, 0), column_ids]]
    scatter-add x1 -> x0, other arithmetic: 13.4 us -> none  [local(): increment = jax.ops.segment_sum(recv_values, recv_slots, num_segments=owned)]
    all_gather x1 -> x0, waiting for transfers between devices: 10.6 us -> none  [local(): charge_col = lax.all_gather(charge_own, 'row', axis=0, tiled=True)]
    select_n x4 -> x0, other arithmetic: 7.1 us -> none  [the longest x1 6.99 us: local(): jnp.where((delays == 0)[:, :, None, None], now_blocks[None], earlier)]
    dot_general x1 -> x0, matrix products: 6.5 us -> none  [local(): jnp.einsum('rkc,rcs->rks', coef_rows, source, preferred_element_type=jnp....]
  transfers between devices with their start and end apart: 6 -> 0, of which waited for: 5 -> 0; matrix products, arithmetic and copies ran while one was open for 22% -> 0% of each run, Pallas kernels for 0% -> 0%
where the time goes in v1:
time: 96.9 us; the launch traced here: 96.6 us
  Pallas kernels  86.7 us (89%)
  local copies, waits for them, and re-layouts  9.17 us (9%)
    pallas_call x1, Pallas kernels, exchange(): pl.pallas_call(exchange_kernel, out_shape=(jax.ShapeDtypeStruct((nodes, E...  51.1 us
    pallas_call x1, Pallas kernels, find_drops(): pl.pallas_call(drops_kernel, out_shape=jax.ShapeDtypeStruct((sowner.shape...  29.7 us
    unnamed x19, local copies, waits for them, and re-layouts  9.17 us
    pallas_call x1, Pallas kernels, current(): pl.pallas_call(current_kernel, out_shape=(jax.ShapeDtypeStruct(acc.shape,...  5.93 us

profile of v1, /device:TPU:1, one launch (start us, length us, event | category | flops | bytes accessed | tf_op | source)
XLA Modules:
  0.0 96.6 jit_solution(12449977283115467932)
XLA Ops:
  0.6 0.0 copy-start.3
  0.6 0.9 copy-done.3
  1.6 0.0 copy-start.4
  1.6 0.7 copy-done.4
  2.3 0.0 copy-start.5
  2.3 0.7 copy-done.5
  2.9 0.0 copy-start.6
  2.9 0.7 copy-done.6
  3.6 0.0 copy-start.7
  3.6 0.7 copy-done.7
  4.3 0.0 copy-start.8
  4.3 0.7 copy-done.8
  5.0 0.0 copy-start
  5.0 51.1 %exchange.1 = (bf16[8192,256]{1,0:T(8,128)(2,1)S(1)}, f32[512,256]{1,0:T(8,128)S(1)}, f32[128,1,128]{2,1,0:T(1,128)S(1)}) custom-call(s32[2,32]{1,0:T(2,128)S(1)} %copy-done.5, f32[256,256]{1,0:T(8,128)S(1)} %copy-done.3, s32[2,256]{1,0:T(2,128)S(1)} %bitcast.6, s32[2,256]{1,0:T(2,128)S(1)} %bitcast.7, s32[2,64]{1,0:T(2,128)S(1)} %bitcast.4, ...), custom_call_target="tpu_custom_call" | custom-call | tf_op jit(solution)/shard_map/exchange/pallas_call | solution.py:320
  56.1 0.0 copy-start.1
  56.1 2.0 %copy-done.1 = bf16[8192,256]{1,0:T(8,128)(2,1)} copy-done((bf16[8192,256]{1,0:T(8,128)(2,1)}, bf16[8192,256]{1,0:T(8,128)(2,1)S(1)}, u32[]{:S(2)}) %copy-start.1) | copy-done | bytes 4194328
  58.1 0.0 copy-done
  58.1 0.0 copy-start.2
  58.1 2.2 %copy-done.2 = bf16[8192,256]{1,0:T(8,128)(2,1)S(1)} copy-done((bf16[8192,256]{1,0:T(8,128)(2,1)S(1)}, bf16[8192,256]{1,0:T(8,128)(2,1)}, u32[]{:S(2)}) %copy-start.2) | copy-done | bytes 4194328
  60.3 5.9 %current.1 = (f32[512,256]{1,0:T(8,128)S(1)}, bf16[8192,256]{1,0:T(8,128)(2,1)}) custom-call(s32[2,32]{1,0:T(2,128)S(1)} %copy-done.5, f32[512,256]{1,0:T(8,128)S(1)} %get-tuple-element.7.acc, bf16[8192,256]{1,0:T(8,128)(2,1)S(1)} %copy-done.2, bf16[512,8192]{1,0:T(8,128)(2,1)S(1)} %copy-done), custom_call_target="tpu_custom_call" | custom-call | tf_op jit(solution)/shard_map/current/pallas_call | solution.py:407
  66.2 29.7 %find_drops.1 = f32[64,256]{1,0:T(8,128)S(1)} custom-call(f32[512,256]{1,0:T(8,128)S(1)} %get-tuple-element.10.part, f32[128,1,128]{2,1,0:T(1,128)S(1)} %get-tuple-element.11.meta, s32[2,64]{1,0:T(2,128)S(1)} %bitcast.5), custom_call_target="tpu_custom_call" | custom-call | tf_op jit(solution)/shard_map/find_drops/pallas_call | solution.py:516
  96.0 0.6 copy.11
Async XLA Ops:
  0.6 1.0 copy-start.3
  1.6 0.7 copy-start.4
  2.3 0.7 copy-start.5
  2.9 0.7 copy-start.6
  3.6 0.7 copy-start.7
  4.3 0.7 copy-start.8
  5.0 53.1 %copy-start = (bf16[512,8192]{1,0:T(8,128)(2,1)S(1)}, bf16[512,8192]{1,0:T(8,128)(2,1)}, u32[]{:S(2)}) copy-start(bf16[512,8192]{1,0:T(8,128)(2,1)} %coef.3) | copy-start | bytes 25165828
  56.1 2.0 %copy-start.1 = (bf16[8192,256]{1,0:T(8,128)(2,1)}, bf16[8192,256]{1,0:T(8,128)(2,1)S(1)}, u32[]{:S(2)}) copy-start(bf16[8192,256]{1,0:T(8,128)(2,1)S(1)} %get-tuple-element.8.charge) | copy-start | bytes 12582916
  58.1 2.2 %copy-start.2 = (bf16[8192,256]{1,0:T(8,128)(2,1)S(1)}, bf16[8192,256]{1,0:T(8,128)(2,1)}, u32[]{:S(2)}) copy-start(bf16[8192,256]{1,0:T(8,128)(2,1)} %copy-done.1) | copy-start | bytes 12582916

commit v2 on v1

v2 whole, which is shorter than its diff:
```python
import functools

import jax
import jax.numpy as jnp
from jax import lax
from jax.experimental import pallas as pl
from jax.experimental.pallas import tpu as pltpu
from jax.sharding import PartitionSpec as P

F32 = jnp.float32
BF16 = jnp.bfloat16
I32 = jnp.int32
MESH = pl.DeviceIdType.MESH

ROWS = 8
COLS = 16
DEV = ROWS * COLS
CORES = 2
XS = ROWS // CORES
BRANCH = 256
CAP = 16
SCAP = 4
OWN = 1024
EXC = 256
HALF = 128
SLOTS = DEV * CAP
BLK = 256
PIECES = 4
PIECE = OWN // PIECES


def iota(shape, dim):
    return lax.broadcasted_iota(I32, shape, dim)


def nn(a, b):
    return lax.dot_general(a, b, (((1,), (0,)), ((), ())), preferred_element_type=F32)


def nt(a, b):
    return lax.dot_general(a, b, (((1,), (1,)), ((), ())), preferred_element_type=F32)


def tn(a, b):
    return lax.dot_general(a, b, (((0,), (0,)), ((), ())), preferred_element_type=F32)


def device_of(index):
    return (index // COLS, lax.rem(index, COLS))


def ranks_of(first, second):
    n = first.shape[1]
    hot_a = iota((DEV, n), 0) == first
    hot_b = iota((DEV, n), 0) == second
    a, b = hot_a.astype(F32), hot_b.astype(F32)
    before = (iota((n, n), 0) < iota((n, n), 1)).astype(BF16)
    seen_a = nn(a.astype(BF16), before)
    seen_b = nn(b.astype(BF16), before) + jnp.sum(a, axis=1, keepdims=True)
    rank_a = jnp.sum(a * seen_a, axis=0, keepdims=True).astype(I32)
    rank_b = jnp.sum(b * seen_b, axis=0, keepdims=True).astype(I32)
    return a.astype(BF16), b.astype(BF16), rank_a, rank_b


def greet(me):
    barrier = pltpu.get_barrier_semaphore()

    def signal(t, _):
        other = lax.rem(me + t, DEV)
        pl.semaphore_signal(barrier, inc=1, device_id=device_of(other), device_id_type=MESH)
        return 0

    lax.fori_loop(1, DEV, signal, 0)
    return barrier


def step_kernel(
    cur_h, owner_h, slot_h, sowner_h, soffset_h, hist, coef_h, delays_h,
    gathered, drops,
    cur, owner, slot, sowner, soffset, delays,
    send, recv, meta_out, meta_in, planes, q_hi, q_lo, past, coef, hist_a, hist_b, acc,
    take, gates, p_send, p_recv, ps_send, ps_recv, answer, replies, as_send, as_recv,
    first_sem, v_send, v_recv, m_send, m_recv, self_sem, past_sem, h_sem, c_sem,
    g_send, g_near, g_pair, r_send, r_recv, rs_send, rs_recv, a_send, a_recv, b_send, b_recv,
):
    row, col = lax.axis_index("row"), lax.axis_index("col")
    me = row * COLS + col
    barrier = greet(me)
    small = ((cur_h, cur), (owner_h, owner), (slot_h, slot), (sowner_h, sowner), (soffset_h, soffset), (delays_h, delays))
    small = [pltpu.make_async_copy(a, b, first_sem.at[n]) for n, (a, b) in enumerate(small)]
    for copy in small:
        copy.start()
    past_copy = pltpu.make_async_copy(hist.at[0, pl.ds(pl.multiple_of(row * OWN, OWN), OWN)], past, past_sem)
    past_copy.start()

    width = 2 * BLK
    steps = coef.shape[0]
    buffers = (hist_a, hist_b)

    def stream(step, which):
        at = pl.ds(pl.multiple_of(step * width, width), width)
        return (
            pltpu.make_async_copy(hist.at[:, at], buffers[which], h_sem.at[which]),
            pltpu.make_async_copy(coef_h.at[:, at], coef.at[step], c_sem.at[which]),
        )

    for which in range(2):
        for copy in stream(which, which):
            copy.start()
    for copy in small:
        copy.wait()

    own = owner[...]
    targets = (own & (ROWS - 1)) * COLS + (own >> 3)
    t_from, t_to = targets[0:1, :], targets[1:2, :]
    hot_from, hot_to, r_from, r_to = ranks_of(t_from, t_to)
    p_from, p_to = t_from * CAP + r_from, t_to * CAP + r_to
    x = cur[...]
    size = jnp.abs(x)
    size = jnp.maximum(size[:, :HALF], size[:, HALF:])
    largest = jnp.max(size.T, axis=0, keepdims=True)
    scale = jnp.full((1, BRANCH), 2.0**-12, F32)
    inverse = jnp.full((1, BRANCH), 2.0**12, F32)
    for _ in range(32):
        smaller = largest <= scale * 16383.0
        scale = jnp.where(smaller, scale * 0.5, scale)
        inverse = jnp.where(smaller, inverse * 2.0, inverse)
    spread = jnp.broadcast_to(inverse, (HALF, BRANCH)).T
    q = jnp.round(x * jnp.concatenate([spread, spread], axis=1))
    high = jnp.floor(q * (1.0 / 256.0))
    q_hi[...] = high.astype(BF16)
    q_lo[...] = (q - high * 256.0).astype(BF16)

    def told(rank, number):
        line = iota((HALF, BRANCH), 0)
        words = jnp.where(line == rank, (number >> 5).astype(F32), 0.0)
        words = words + jnp.where(line == rank + 16, (number & 31).astype(F32), 0.0)
        return (words + jnp.where(line == rank + 32, scale, 0.0)).astype(BF16)

    s_own, s_off = sowner[...], soffset[...]
    s_from, s_to = s_own[0:1, :], s_own[1:2, :]
    hot_0, hot_1, s_0, s_1 = ranks_of(s_from, s_to)

    def asked(rank, offset):
        line = iota((HALF, offset.shape[1]), 0)
        return jnp.where(line == rank + 48, offset.astype(F32), 0.0).astype(BF16)

    slots = slot[...]
    words = nt(hot_from, told(r_from, slots[0:1, :])) + nt(hot_to, told(r_to, slots[1:2, :]))
    words = words + nt(hot_0, asked(s_0, s_off[0:1, :])) + nt(hot_1, asked(s_1, s_off[1:2, :]))
    meta_out[...] = words.reshape(DEV, 1, HALF)

    chunk = 256

    def word_of(value):
        return (value[:, :HALF] << 16) | (value[:, HALF:] & 0xFFFF)

    def fill(t, _):
        place = iota((chunk, BRANCH), 0) + t * chunk
        sign = (place == p_to).astype(F32) - (place == p_from).astype(F32)
        sign = sign.astype(BF16)
        value = (nn(sign, q_hi[...]) * 256.0 + nn(sign, q_lo[...])).astype(I32)
        send[pl.ds(pl.multiple_of(t * chunk, chunk), chunk), :] = word_of(value)
        return 0

    lax.fori_loop(0, SLOTS // chunk, fill, 0)

    pl.semaphore_wait(barrier, DEV - 1)

    def chunk_of(index):
        return pl.ds(pl.multiple_of(index * CAP, CAP), CAP)

    def out(t, _):
        other = lax.rem(me + t, DEV)
        pltpu.make_async_remote_copy(
            meta_out.at[other], meta_in.at[me], m_send, m_recv,
            device_id=device_of(other), device_id_type=MESH,
        ).start()
        pltpu.make_async_remote_copy(
            send.at[chunk_of(other)], recv.at[chunk_of(me)], v_send, v_recv,
            device_id=device_of(other), device_id_type=MESH,
        ).start()
        return 0

    lax.fori_loop(1, DEV, out, 0)
    self_v = pltpu.make_async_copy(send.at[chunk_of(me)], recv.at[chunk_of(me)], self_sem.at[0])
    self_m = pltpu.make_async_copy(meta_out.at[me], meta_in.at[me], self_sem.at[1])
    self_v.start()
    self_m.start()

    span = 2 * SCAP
    asks = DEV * span
    line = iota((asks, s_own.shape[1]), 0)
    gate = (line == s_from * span + s_0).astype(F32) - (line == s_to * span + s_1).astype(F32)
    gates[...] = gate.astype(BF16)

    acc[...] = jnp.zeros_like(acc)

    def delayed(pair, _):
        for which in range(2):
            step = pair * 2 + which
            for copy in stream(step, which):
                copy.wait()
            h = buffers[which]
            for i in range(2):
                total = acc[pl.ds(i * BLK, BLK), :]
                for k in range(2):
                    d = delays[i, step * 2 + k]
                    source = h[jnp.maximum(d - 1, 0), pl.ds(k * BLK, BLK), :]
                    part = nn(coef[step, pl.ds(i * BLK, BLK), pl.ds(k * BLK, BLK)], source)
                    total = total + jnp.where(d > 0, part, 0.0)
                acc[pl.ds(i * BLK, BLK), :] = total

            @pl.when(pair < steps // 2 - 1)
            def _():
                for copy in stream(step + 2, which):
                    copy.start()

        return 0

    lax.fori_loop(0, steps // 2, delayed, 0)

    self_m.wait()
    rest = pl.ds(0, DEV - 1)
    pltpu.make_async_copy(meta_in.at[rest], meta_in.at[rest], m_recv).wait()
    heard = meta_in[...].reshape(DEV, HALF).astype(BF16)
    expand = ((iota((DEV, SLOTS), 1) >> 4) == iota((DEV, SLOTS), 0)).astype(BF16)
    wide = tn(heard, expand)
    line = iota((16, SLOTS), 0)
    mine = line == (iota((16, SLOTS), 1) & 15)

    def picked(first):
        return jnp.sum(jnp.where(mine, wide[first : first + 16, :], 0.0), axis=0, keepdims=True)

    node = (picked(0) * 32.0 + picked(16)).astype(I32)
    weight = picked(32)

    share = acc.shape[0] // COLS
    expand = ((iota((DEV, asks), 1) >> 3) == iota((DEV, asks), 0)).astype(BF16)
    wide = tn(heard, expand)[48:56, :]
    line = iota((span, asks), 0)
    mine = line == (iota((span, asks), 1) & (span - 1))
    place = jnp.sum(jnp.where(mine, wide, 0.0), axis=0, keepdims=True).astype(I32)
    take[...] = (iota((share, asks), 0) == place).astype(BF16)

    self_v.wait()
    rest = pl.ds(0, (DEV - 1) * CAP)
    pltpu.make_async_copy(recv.at[rest], recv.at[rest], v_recv).wait()

    def unpack(t, _):
        at = pl.ds(pl.multiple_of(t * chunk, chunk), chunk)
        w = recv[at, :]
        planes[at, 0 * HALF : 1 * HALF] = (w >> 24).astype(F32).astype(BF16)
        planes[at, 1 * HALF : 2 * HALF] = ((w << 16) >> 24).astype(F32).astype(BF16)
        planes[at, 2 * HALF : 3 * HALF] = ((w >> 16) & 255).astype(F32).astype(BF16)
        planes[at, 3 * HALF : 4 * HALF] = (w & 255).astype(F32).astype(BF16)
        return 0

    lax.fori_loop(0, SLOTS // chunk, unpack, 0)
    past_copy.wait()

    xpos, core = row // CORES, lax.rem(row, CORES)
    right, left, far = lax.rem(xpos + 1, XS), lax.rem(xpos + XS - 1, XS), lax.rem(xpos + 2, XS)
    other = 1 - core

    def piece(at_x, at_core, j):
        start = (at_x * CORES + at_core) * OWN + j * PIECE
        return pl.ds(pl.multiple_of(start, PIECE), PIECE)

    def move(at_x, at_core, j, to_x, to_core, sem, recv_sem):
        at = piece(at_x, at_core, j)
        return pltpu.make_async_remote_copy(
            gathered.at[at], gathered.at[at], sem, recv_sem,
            device_id=(to_x * CORES + to_core, col), device_id_type=MESH,
        )

    def arrived(at_x, at_core, j, recv_sem):
        at = piece(at_x, at_core, j)
        pltpu.make_async_copy(gathered.at[at], gathered.at[at], recv_sem).wait()

    def use(at_x, at_core, j):
        block = (at_x * CORES + at_core) * PIECES + j
        source = gathered[piece(at_x, at_core, j), :]
        at = pl.ds(pl.multiple_of(lax.rem(j, 2) * BLK, BLK), BLK)
        for i in range(2):
            part = nn(coef[block // 2, pl.ds(i * BLK, BLK), at], source)
            acc[pl.ds(i * BLK, BLK), :] += jnp.where(delays[i, block] == 0, part, 0.0)

    def turn(t):
        return lax.rem(t, 2) * 2 + t // 2

    def settle(t, _):
        j = turn(t)
        spot = iota((PIECE, SLOTS), 0) + j * PIECE
        gate = jnp.where(spot == node, weight, 0.0).astype(BF16)
        both = nn(gate, planes[...])
        rise = both[:, :EXC] * 256.0 + both[:, EXC:]
        fresh = past[pl.ds(pl.multiple_of(j * PIECE, PIECE), PIECE), :].astype(F32) + rise
        gathered[piece(xpos, core, j), :] = fresh.astype(BF16)
        move(xpos, core, j, right, core, g_send.at[0, j], g_near.at[0, j]).start()
        move(xpos, core, j, left, core, g_send.at[1, j], g_near.at[1, j]).start()
        move(xpos, core, j, xpos, other, g_send.at[2, j], g_pair.at[0, j]).start()
        return 0

    lax.fori_loop(0, PIECES, settle, 0)

    def near(t, _):
        j = turn(t)
        arrived(left, core, j, g_near.at[0, j])

        @pl.when(j < 2)
        def _():
            move(left, core, j, right, core, g_send.at[3, j], g_near.at[2, j]).start()

        move(left, core, j, xpos, other, g_send.at[4, j], g_pair.at[1, j]).start()
        use(xpos, core, j)
        arrived(right, core, j, g_near.at[1, j])

        @pl.when(j >= 2)
        def _():
            move(right, core, j, left, core, g_send.at[3, j], g_near.at[2, j]).start()

        move(right, core, j, xpos, other, g_send.at[5, j], g_pair.at[2, j]).start()
        use(left, core, j)
        use(right, core, j)
        arrived(xpos, other, j, g_pair.at[0, j])
        use(xpos, other, j)
        return 0

    lax.fori_loop(0, PIECES, near, 0)

    def distant(t, _):
        j = turn(t)
        arrived(far, core, j, g_near.at[2, j])
        move(far, core, j, xpos, other, g_send.at[6, j], g_pair.at[3, j]).start()
        arrived(left, other, j, g_pair.at[1, j])
        use(left, other, j)
        arrived(right, other, j, g_pair.at[2, j])
        use(right, other, j)
        use(far, core, j)
        return 0

    lax.fori_loop(0, PIECES, distant, 0)

    def last(t, _):
        j = turn(t)
        arrived(far, other, j, g_pair.at[3, j])
        use(far, other, j)
        return 0

    lax.fori_loop(0, PIECES, last, 0)

    def rows_of(index):
        return pl.ds(pl.multiple_of(index * share, share), share)

    def coded(value, top):
        number = jnp.round(value * (32767.0 / jnp.maximum(top, 1e-30)))
        return number

    def give(t, _):
        to = lax.rem(col + t, COLS)
        value = acc[rows_of(to), :]
        top = jnp.max(jnp.abs(value), axis=0, keepdims=True)
        p_send[rows_of(to), :] = word_of(coded(value, top).astype(I32))
        ps_send[to, 0:1, :] = top[:, :HALF]
        ps_send[to, 1:2, :] = top[:, HALF:]

        @pl.when(t < COLS)
        def _():
            pltpu.make_async_remote_copy(
                ps_send.at[to], ps_recv.at[col], rs_send, rs_recv,
                device_id=(row, to), device_id_type=MESH,
            ).start()
            pltpu.make_async_remote_copy(
                p_send.at[rows_of(to)], p_recv.at[rows_of(col)], r_send, r_recv,
                device_id=(row, to), device_id_type=MESH,
            ).start()

        return 0

    lax.fori_loop(1, COLS + 1, give, 0)
    self_p = pltpu.make_async_copy(p_send.at[rows_of(col)], p_recv.at[rows_of(col)], self_sem.at[2])
    self_s = pltpu.make_async_copy(ps_send.at[col], ps_recv.at[col], self_sem.at[3])
    self_p.start()
    self_s.start()
    self_p.wait()
    self_s.wait()
    rest = pl.ds(0, COLS - 1)
    pltpu.make_async_copy(ps_recv.at[rest], ps_recv.at[rest], rs_recv).wait()
    rest = pl.ds(0, (COLS - 1) * share)
    pltpu.make_async_copy(p_recv.at[rest], p_recv.at[rest], r_recv).wait()

    def gain(n, totals):
        w = p_recv[rows_of(n), :]
        top = ps_recv[n] * (1.0 / 32767.0)
        a = totals[0] + (w >> 16).astype(F32) * top[0:1, :]
        b = totals[1] + ((w << 16) >> 16).astype(F32) * top[1:2, :]
        return a, b

    zero = jnp.zeros((share, HALF), F32)
    a, b = lax.fori_loop(0, COLS, gain, (zero, zero))

    top = jnp.max(jnp.maximum(jnp.abs(a), jnp.abs(b)), axis=0, keepdims=True)
    as_send[...] = top.reshape(1, 1, HALF)
    number = jnp.concatenate([coded(a, top), coded(b, top)], axis=1)
    high = jnp.floor(number * (1.0 / 256.0))
    low = (number - high * 256.0).astype(BF16)
    high = high.astype(BF16)
    for g in range(asks // HALF):
        chosen = take[:, g * HALF : (g + 1) * HALF]
        value = (tn(chosen, high) * 256.0 + tn(chosen, low)).astype(I32)
        word = word_of(value).reshape(HALF // span, span, HALF)
        answer[pl.ds(g * (HALF // span), HALF // span)] = word[:, :SCAP, :]

    def send_answer(t, _):
        to = lax.rem(me + t, DEV)
        pltpu.make_async_remote_copy(
            as_send.at[0], as_recv.at[me], b_send, b_recv,
            device_id=device_of(to), device_id_type=MESH,
        ).start()
        pltpu.make_async_remote_copy(
            answer.at[to], replies.at[me], a_send, a_recv,
            device_id=device_of(to), device_id_type=MESH,
        ).start()
        return 0

    lax.fori_loop(1, DEV, send_answer, 0)
    self_a = pltpu.make_async_copy(answer.at[me], replies.at[me], self_sem.at[4])
    self_b = pltpu.make_async_copy(as_send.at[0], as_recv.at[me], self_sem.at[5])
    self_a.start()
    self_b.start()

    for n in range(7):
        def left_here(j, _):
            at = piece(xpos, core, j)
            pltpu.make_async_copy(gathered.at[at], gathered.at[at], g_send.at[n, j]).wait()
            return 0

        lax.fori_loop(0, PIECES, left_here, 0)
    rest = pl.ds(0, DEV - 1)
    pltpu.make_async_copy(meta_out.at[rest], meta_out.at[rest], m_send).wait()
    rest = pl.ds(0, (DEV - 1) * CAP)
    pltpu.make_async_copy(send.at[rest], send.at[rest], v_send).wait()
    rest = pl.ds(0, COLS - 1)
    pltpu.make_async_copy(ps_send.at[rest], ps_send.at[rest], rs_send).wait()
    rest = pl.ds(0, (COLS - 1) * share)
    pltpu.make_async_copy(p_send.at[rest], p_send.at[rest], r_send).wait()

    self_a.wait()
    self_b.wait()
    rest = pl.ds(0, DEV - 1)
    pltpu.make_async_copy(as_recv.at[rest], as_recv.at[rest], b_recv).wait()
    pltpu.make_async_copy(replies.at[rest], replies.at[rest], a_recv).wait()
    w = replies[...]
    top = as_recv[...] * (1.0 / 32767.0)
    picks = gates[...]
    for half in range(2):
        number = (w >> 16) if half == 0 else ((w << 16) >> 16)
        value = number.astype(F32) * top
        value = jnp.concatenate([value, value], axis=1).reshape(asks, HALF)
        high, low = split(value)
        drops[:, half * HALF : (half + 1) * HALF] = tn(picks, high) + tn(picks, low)
    pltpu.make_async_copy(as_recv.at[rest], as_recv.at[rest], b_send).wait()
    pltpu.make_async_copy(answer.at[rest], answer.at[rest], a_send).wait()


def split(value):
    top = value.astype(BF16)
    return top, (value - top.astype(F32)).astype(BF16)


def step(cur, owner, slot, sowner, soffset, hist, coef, delays):
    vmem, hbm = pl.BlockSpec(memory_space=pltpu.VMEM), pl.BlockSpec(memory_space=pltpu.HBM)
    nodes, rows = hist.shape[1], coef.shape[0]
    width = 2 * BLK
    dma = pltpu.SemaphoreType.DMA
    asks = DEV * 2 * SCAP
    return pl.pallas_call(
        step_kernel,
        out_shape=(
            jax.ShapeDtypeStruct((nodes, EXC), BF16),
            jax.ShapeDtypeStruct((sowner.shape[1], EXC), F32),
        ),
        in_specs=[hbm] * 8,
        out_specs=(vmem, vmem),
        scratch_shapes=[
            pltpu.VMEM(cur.shape, F32),
            pltpu.VMEM(owner.shape, I32),
            pltpu.VMEM(slot.shape, I32),
            pltpu.VMEM(sowner.shape, I32),
            pltpu.VMEM(soffset.shape, I32),
            pltpu.SMEM(delays.shape, I32),
            pltpu.VMEM((SLOTS, HALF), I32),
            pltpu.VMEM((SLOTS, HALF), I32),
            pltpu.VMEM((DEV, 1, HALF), F32),
            pltpu.VMEM((DEV, 1, HALF), F32),
            pltpu.VMEM((SLOTS, 2 * EXC), BF16),
            pltpu.VMEM((BRANCH, EXC), BF16),
            pltpu.VMEM((BRANCH, EXC), BF16),
            pltpu.VMEM((OWN, EXC), BF16),
            pltpu.VMEM((nodes // width, rows, width), BF16),
            pltpu.VMEM((4, width, EXC), BF16),
            pltpu.VMEM((4, width, EXC), BF16),
            pltpu.VMEM((rows, EXC), F32),
            pltpu.VMEM((rows // COLS, asks), BF16),
            pltpu.VMEM((asks, sowner.shape[1]), BF16),
            pltpu.VMEM((rows, HALF), I32),
            pltpu.VMEM((rows, HALF), I32),
            pltpu.VMEM((COLS, 2, HALF), F32),
            pltpu.VMEM((COLS, 2, HALF), F32),
            pltpu.VMEM((DEV, SCAP, HALF), I32),
            pltpu.VMEM((DEV, SCAP, HALF), I32),
            pltpu.VMEM((1, 1, HALF), F32),
            pltpu.VMEM((DEV, 1, HALF), F32),
            dma((6,)), dma, dma, dma, dma, dma((6,)), dma, dma((2,)), dma((2,)),
            dma((7, PIECES)), dma((3, PIECES)), dma((4, PIECES)),
            dma, dma, dma, dma, dma, dma, dma, dma,
        ],
        compiler_params=pltpu.CompilerParams(
            collective_id=0, has_side_effects=True, vmem_limit_bytes=52 << 20
        ),
        name="step",
    )(cur, owner, slot, sowner, soffset, hist, coef, delays)


def local(
    currents, branch_owner, branch_slot, history, coefficients, delays, slab_owner, slab_offset
):
    return step(
        currents, branch_owner.T, branch_slot.T, slab_owner.T, slab_offset.T, history, coefficients, delays
    )


def solution(mesh):
    placed = (
        P(("row", "col"), None),
        P(("row", "col"), None),
        P(("row", "col"), None),
        P(None, "col", None),
        P("row", "col"),
        P("row", "col"),
        P(("row", "col"), None),
        P(("row", "col"), None),
    )
    return jax.shard_map(
        local,
        mesh=mesh,
        in_specs=placed,
        out_specs=(P("col", None), P(("row", "col"), None)),
        check_vma=False,
    )
```

time: 96.9 us -> 78.9 us (0.81)
  Pallas kernels: 86.7 us -> 68.4 us
    pallas_call x3 -> x1, Pallas kernels: 86.7 us -> 68.4 us  [step(): pl.pallas_call(step_kernel, out_shape=(jax.ShapeDtypeStruct((nodes, EXC),...]
    unnamed x19 -> x14, local copies, waits for them, and re-layouts: 9.17 us -> 9.44 us
where the time goes in v2:
time: 78.9 us; the launch traced here: 78.5 us
  Pallas kernels  68.4 us (87%)
  local copies, waits for them, and re-layouts  9.44 us (12%)
    pallas_call x1, Pallas kernels, step(): pl.pallas_call(step_kernel, out_shape=(jax.ShapeDtypeStruct((nodes, EXC),...  68.4 us
    unnamed x14, local copies, waits for them, and re-layouts  9.44 us

profile of v2, /device:TPU:1, one launch (start us, length us, event | category | flops | bytes accessed | tf_op | source)
XLA Modules:
  0.0 78.5 jit_solution(14840638849091167545)
XLA Ops:
  0.6 0.0 copy-start
  0.6 0.9 %copy-done = f32[256,256]{1,0:T(8,128)S(1)} copy-done((f32[256,256]{1,0:T(8,128)S(1)}, f32[256,256]{1,0:T(8,128)}, u32[]{:S(2)}) %copy-start) | copy-done | bytes 262168
  1.6 0.0 copy-start.1
  1.6 0.7 copy-done.1
  2.3 0.0 copy-start.2
  2.3 0.7 copy-done.2
  2.9 0.0 copy-start.3
  3.0 0.7 copy-done.3
  3.6 0.0 copy-start.4
  3.6 0.7 copy-done.4
  4.3 0.0 copy-start.5
  4.3 0.7 copy-done.5
  5.0 68.4 %step.1 = (bf16[8192,256]{1,0:T(8,128)(2,1)}, f32[64,256]{1,0:T(8,128)S(1)}) custom-call(f32[256,256]{1,0:T(8,128)S(1)} %copy-done, s32[2,256]{1,0:T(2,128)S(1)} %bitcast.4, s32[2,256]{1,0:T(2,128)S(1)} %bitcast.5, s32[2,64]{1,0:T(2,128)S(1)} %bitcast.6, s32[2,64]{1,0:T(2,128)S(1)} %bitcast.7, bf16[4,8192,256]{2,1,0:T(8,128)(2,1)} %hist.1, ...), custom_call_target="tpu_custom_call" | custom-call | tf_op jit(solution)/shard_map/step/pallas_call | solution.py:478
  73.4 4.5 %copy.12 = bf16[8192,256]{1,0:T(8,128)(2,1)} copy(bf16[8192,256]{1,0:T(8,128)(2,1)} %get-tuple-element.4) | data formatting | bytes 8388608
  77.9 0.6 copy.13
Async XLA Ops:
  0.6 1.0 %copy-start = (f32[256,256]{1,0:T(8,128)S(1)}, f32[256,256]{1,0:T(8,128)}, u32[]{:S(2)}) copy-start(f32[256,256]{1,0:T(8,128)} %cur_h.1) | copy-start | bytes 786436
  1.6 0.7 copy-start.1
  2.3 0.7 copy-start.2
  2.9 0.7 copy-start.3
  3.6 0.7 copy-start.4
  4.3 0.7 copy-start.5

commit v3 on v2

v3 whole, which is shorter than its diff:
```python
import functools

import jax
import jax.numpy as jnp
from jax import lax
from jax.experimental import pallas as pl
from jax.experimental.pallas import tpu as pltpu
from jax.sharding import PartitionSpec as P

F32 = jnp.float32
BF16 = jnp.bfloat16
I32 = jnp.int32
MESH = pl.DeviceIdType.MESH

ROWS = 8
COLS = 16
DEV = ROWS * COLS
CORES = 2
XS = ROWS // CORES
BRANCH = 256
CAP = 16
SCAP = 4
OWN = 1024
EXC = 256
HALF = 128
SLOTS = DEV * CAP
BLK = 256
PIECES = 4
PIECE = OWN // PIECES
FULL = 67043328
STRIDE = 1
LEAST = 2.0**-80


def iota(shape, dim):
    return lax.broadcasted_iota(I32, shape, dim)


def nn(a, b):
    return lax.dot_general(a, b, (((1,), (0,)), ((), ())), preferred_element_type=F32)


def nt(a, b):
    return lax.dot_general(a, b, (((1,), (1,)), ((), ())), preferred_element_type=F32)


def tn(a, b):
    return lax.dot_general(a, b, (((0,), (0,)), ((), ())), preferred_element_type=F32)


def power(exponent, sign):
    result = jnp.ones(exponent.shape, F32)
    for bit in range(7):
        factor = 2.0 ** (sign * (1 << bit))
        result = result * jnp.where(((exponent >> bit) & 1) > 0, factor, 1.0)
    return result


def coded(value, top):
    up = jnp.zeros(top.shape, I32)
    unit = jnp.full(top.shape, LEAST, F32)
    inverse = jnp.full(top.shape, 1.0 / LEAST, F32)
    for bit in (6, 5, 4, 3, 2, 1, 0):
        leap = 1 << bit
        larger = top > unit * (32766.0 * 2.0 ** (leap - 1))
        up = jnp.where(larger, up + leap, up)
        unit = jnp.where(larger, unit * 2.0**leap, unit)
        inverse = jnp.where(larger, inverse * 2.0**-leap, inverse)
    return up, jnp.round(value * inverse)


def device_of(index):
    return (index // COLS, lax.rem(index, COLS))


def ranks_of(first, second):
    n = first.shape[1]
    hot_a = iota((DEV, n), 0) == first
    hot_b = iota((DEV, n), 0) == second
    a, b = hot_a.astype(F32), hot_b.astype(F32)
    before = (iota((n, n), 0) < iota((n, n), 1)).astype(BF16)
    seen_a = nn(a.astype(BF16), before)
    seen_b = nn(b.astype(BF16), before) + jnp.sum(a, axis=1, keepdims=True)
    rank_a = jnp.sum(a * seen_a, axis=0, keepdims=True).astype(I32)
    rank_b = jnp.sum(b * seen_b, axis=0, keepdims=True).astype(I32)
    return a.astype(BF16), b.astype(BF16), rank_a, rank_b


def greet(me):
    barrier = pltpu.get_barrier_semaphore()

    def signal(t, _):
        other = lax.rem(me + t, DEV)
        pl.semaphore_signal(barrier, inc=1, device_id=device_of(other), device_id_type=MESH)
        return 0

    lax.fori_loop(1, DEV, signal, 0)
    return barrier


def step_kernel(
    cur_h, owner_h, slot_h, sowner_h, soffset_h, hist, coef_h, delays_h,
    charge_out, replies,
    cur, owner, slot, sowner, soffset, delays,
    send, recv, planes, q_hi, q_lo, past, coef, held, acc, gathered,
    take, p_send, p_recv, answer,
    first_sem, v_send, v_recv, self_sem, past_sem, h_sem, c_sem, w_sem,
    g_send, g_near, g_pair, r_send, r_recv, a_send, a_recv,
):
    row, col = lax.axis_index("row"), lax.axis_index("col")
    me = row * COLS + col
    barrier = greet(me)
    small = ((cur_h, cur), (owner_h, owner), (slot_h, slot), (sowner_h, sowner), (soffset_h, soffset), (delays_h, delays))
    small = [pltpu.make_async_copy(a, b, first_sem.at[n]) for n, (a, b) in enumerate(small)]
    for copy in small:
        copy.start()
    past_copy = pltpu.make_async_copy(hist.at[0, pl.ds(pl.multiple_of(row * OWN, OWN), OWN)], past, past_sem)
    past_copy.start()

    width = 2 * BLK
    steps = coef.shape[0]

    def fetch(step):
        at = pl.ds(pl.multiple_of(step * width, width), width)
        return (
            pltpu.make_async_copy(hist.at[:, at], held.at[:, at], h_sem),
            pltpu.make_async_copy(coef_h.at[:, at], coef.at[step], c_sem.at[step]),
        )

    def bring(step, _):
        for copy in fetch(step):
            copy.start()
        return 0

    lax.fori_loop(0, steps, bring, 0)
    for copy in small:
        copy.wait()

    own = owner[...]
    targets = (own & (ROWS - 1)) * COLS + (own >> 3)
    t_from, t_to = targets[0:1, :], targets[1:2, :]
    hot_from, hot_to, r_from, r_to = ranks_of(t_from, t_to)
    p_from, p_to = t_from * CAP + r_from, t_to * CAP + r_to
    x = cur[...]
    size = jnp.abs(x)
    size = jnp.maximum(size[:, :HALF], size[:, HALF:])
    largest = jnp.max(size.T, axis=0, keepdims=True)
    scale = jnp.full((1, BRANCH), 2.0**-12, F32)
    inverse = jnp.full((1, BRANCH), 2.0**12, F32)
    exponent = jnp.ones((1, BRANCH), F32)
    for _ in range(32):
        smaller = largest <= scale * 16383.0
        scale = jnp.where(smaller, scale * 0.5, scale)
        inverse = jnp.where(smaller, inverse * 2.0, inverse)
        exponent = jnp.where(smaller, exponent + 1.0, exponent)
    spread = jnp.broadcast_to(inverse, (HALF, BRANCH)).T
    q = jnp.round(x * jnp.concatenate([spread, spread], axis=1))
    high = jnp.floor(q * (1.0 / 256.0))
    q_hi[...] = high.astype(BF16)
    q_lo[...] = (q - high * 256.0).astype(BF16)

    def told(rank, number):
        line = iota((HALF, BRANCH), 0)
        words = jnp.where(line == rank, (number >> 5).astype(F32), 0.0)
        words = words + jnp.where(line == rank + 16, (number & 31).astype(F32), 0.0)
        return (words + jnp.where(line == rank + 32, exponent, 0.0)).astype(BF16)

    s_own, s_off = sowner[...], soffset[...]
    s_from, s_to = s_own[0:1, :], s_own[1:2, :]
    hot_0, hot_1, s_0, s_1 = ranks_of(s_from, s_to)

    def asked(rank, offset):
        line = iota((HALF, offset.shape[1]), 0)
        return jnp.where(line == rank + 48, offset.astype(F32), 0.0).astype(BF16)

    slots = slot[...]
    words = nt(hot_from, told(r_from, slots[0:1, :])) + nt(hot_to, told(r_to, slots[1:2, :]))
    words = words + nt(hot_0, asked(s_0, s_off[0:1, :])) + nt(hot_1, asked(s_1, s_off[1:2, :]))
    send[:, CAP : CAP + 1, :] = words.astype(I32).reshape(DEV, 1, HALF)

    chunk = 256

    def word_of(value):
        return (value[:, :HALF] << 16) | (value[:, HALF:] & 0xFFFF)

    def fill(t, _):
        place = iota((chunk, BRANCH), 0) + t * chunk
        sign = (place == p_to).astype(F32) - (place == p_from).astype(F32)
        sign = sign.astype(BF16)
        value = (nn(sign, q_hi[...]) * 256.0 + nn(sign, q_lo[...])).astype(I32)
        word = word_of(value).reshape(chunk // CAP, CAP, HALF)
        send[pl.ds(t * (chunk // CAP), chunk // CAP), 0:CAP, :] = word
        return 0

    lax.fori_loop(0, SLOTS // chunk, fill, 0)

    pl.semaphore_wait(barrier, DEV - 1)

    def out(t, _):
        other = lax.rem(me + t * STRIDE, DEV)
        pltpu.make_async_remote_copy(
            send.at[other], recv.at[me], v_send, v_recv,
            device_id=device_of(other), device_id_type=MESH,
        ).start()
        return 0

    lax.fori_loop(1, DEV, out, 0)
    self_v = pltpu.make_async_copy(send.at[me], recv.at[me], self_sem.at[0])
    self_v.start()
    span = 2 * SCAP
    asks = DEV * span

    acc[...] = jnp.zeros_like(acc)

    def landed(step, _):
        for copy in fetch(step):
            copy.wait()
        return 0

    lax.fori_loop(0, steps, landed, 0)

    def delayed(step, _):
        for i in range(2):
            total = acc[pl.ds(i * BLK, BLK), :]
            for k in range(2):
                d = delays[i, step * 2 + k]
                at = pl.ds(pl.multiple_of(step * width + k * BLK, BLK), BLK)
                source = held[jnp.maximum(d - 1, 0), at, :]
                part = nn(coef[step, pl.ds(i * BLK, BLK), pl.ds(k * BLK, BLK)], source)
                total = total + jnp.where(d > 0, part, 0.0)
            acc[pl.ds(i * BLK, BLK), :] = total
        return 0

    lax.fori_loop(0, steps, delayed, 0)

    self_v.wait()
    rest = pl.ds(0, DEV - 1)
    pltpu.make_async_copy(recv.at[rest], recv.at[rest], v_recv).wait()
    heard = recv[:, CAP : CAP + 1, :].reshape(DEV, HALF).astype(F32).astype(BF16)
    expand = ((iota((DEV, SLOTS), 1) >> 4) == iota((DEV, SLOTS), 0)).astype(BF16)
    wide = tn(heard, expand)
    line = iota((16, SLOTS), 0)
    mine = line == (iota((16, SLOTS), 1) & 15)

    def picked(first):
        return jnp.sum(jnp.where(mine, wide[first : first + 16, :], 0.0), axis=0, keepdims=True)

    node = (picked(0) * 32.0 + picked(16)).astype(I32)
    weight = picked(32).astype(I32)
    weight = jnp.where(weight > 0, power(weight - 1, -1) * 2.0**-12, 0.0)

    share = acc.shape[0] // COLS
    expand = ((iota((DEV, asks), 1) >> 3) == iota((DEV, asks), 0)).astype(BF16)
    wide = tn(heard, expand)[48:56, :]
    line = iota((span, asks), 0)
    mine = line == (iota((span, asks), 1) & (span - 1))
    place = jnp.sum(jnp.where(mine, wide, 0.0), axis=0, keepdims=True).astype(I32)
    take[...] = (iota((share, asks), 0) == place).astype(BF16)

    def unpack(t, _):
        at = pl.ds(pl.multiple_of(t * chunk, chunk), chunk)
        w = recv[pl.ds(t * (chunk // CAP), chunk // CAP), 0:CAP, :].reshape(chunk, HALF)
        planes[at, 0 * HALF : 1 * HALF] = (w >> 24).astype(F32).astype(BF16)
        planes[at, 1 * HALF : 2 * HALF] = ((w << 16) >> 24).astype(F32).astype(BF16)
        planes[at, 2 * HALF : 3 * HALF] = ((w >> 16) & 255).astype(F32).astype(BF16)
        planes[at, 3 * HALF : 4 * HALF] = (w & 255).astype(F32).astype(BF16)
        return 0

    lax.fori_loop(0, SLOTS // chunk, unpack, 0)
    past_copy.wait()

    xpos, core = row // CORES, lax.rem(row, CORES)
    right, left, far = lax.rem(xpos + 1, XS), lax.rem(xpos + XS - 1, XS), lax.rem(xpos + 2, XS)
    other = 1 - core

    def piece(at_x, at_core, j):
        start = (at_x * CORES + at_core) * OWN + j * PIECE
        return pl.ds(pl.multiple_of(start, PIECE), PIECE)

    def move(at_x, at_core, j, to_x, to_core, sem, recv_sem):
        at = piece(at_x, at_core, j)
        return pltpu.make_async_remote_copy(
            gathered.at[at], gathered.at[at], sem, recv_sem,
            device_id=(to_x * CORES + to_core, col), device_id_type=MESH,
        )

    def arrived(at_x, at_core, j, recv_sem):
        at = piece(at_x, at_core, j)
        pltpu.make_async_copy(gathered.at[at], gathered.at[at], recv_sem).wait()

    def write(at_x, at_core, j):
        at = piece(at_x, at_core, j)
        return pltpu.make_async_copy(gathered.at[at], charge_out.at[at], w_sem.at[at_x * CORES + at_core, j])

    def use(at_x, at_core, j):
        block = (at_x * CORES + at_core) * PIECES + j
        write(at_x, at_core, j).start()
        source = gathered[piece(at_x, at_core, j), :]
        at = pl.ds(pl.multiple_of(lax.rem(j, 2) * BLK, BLK), BLK)
        for i in range(2):
            part = nn(coef[block // 2, pl.ds(i * BLK, BLK), at], source)
            acc[pl.ds(i * BLK, BLK), :] += jnp.where(delays[i, block] == 0, part, 0.0)

    def turn(t):
        return lax.rem(t, 2) * 2 + t // 2

    def settle(t, _):
        j = turn(t)
        spot = iota((PIECE, SLOTS), 0) + j * PIECE
        gate = jnp.where(spot == node, weight, 0.0).astype(BF16)
        both = nn(gate, planes[...])
        rise = both[:, :EXC] * 256.0 + both[:, EXC:]
        fresh = past[pl.ds(pl.multiple_of(j * PIECE, PIECE), PIECE), :].astype(F32) + rise
        gathered[piece(xpos, core, j), :] = fresh.astype(BF16)
        move(xpos, core, j, right, core, g_send.at[0, j], g_near.at[0, j]).start()
        move(xpos, core, j, left, core, g_send.at[1, j], g_near.at[1, j]).start()
        move(xpos, core, j, xpos, other, g_send.at[2, j], g_pair.at[0, j]).start()
        return 0

    lax.fori_loop(0, PIECES, settle, 0)

    def near(t, _):
        j = turn(t)
        arrived(left, core, j, g_near.at[0, j])

        @pl.when(j < 2)
        def _():
            move(left, core, j, right, core, g_send.at[3, j], g_near.at[2, j]).start()

        move(left, core, j, xpos, other, g_send.at[4, j], g_pair.at[1, j]).start()
        use(xpos, core, j)
        arrived(right, core, j, g_near.at[1, j])

        @pl.when(j >= 2)
        def _():
            move(right, core, j, left, core, g_send.at[3, j], g_near.at[2, j]).start()

        move(right, core, j, xpos, other, g_send.at[5, j], g_pair.at[2, j]).start()
        use(left, core, j)
        use(right, core, j)
        arrived(xpos, other, j, g_pair.at[0, j])
        use(xpos, other, j)
        return 0

    lax.fori_loop(0, PIECES, near, 0)

    def distant(t, _):
        j = turn(t)
        arrived(far, core, j, g_near.at[2, j])
        move(far, core, j, xpos, other, g_send.at[6, j], g_pair.at[3, j]).start()
        arrived(left, other, j, g_pair.at[1, j])
        use(left, other, j)
        arrived(right, other, j, g_pair.at[2, j])
        use(right, other, j)
        use(far, core, j)
        return 0

    lax.fori_loop(0, PIECES, distant, 0)

    def last(t, _):
        j = turn(t)
        arrived(far, other, j, g_pair.at[3, j])
        use(far, other, j)
        return 0

    lax.fori_loop(0, PIECES, last, 0)

    def give(t, _):
        to = lax.rem(col + t, COLS)
        value = acc[pl.ds(pl.multiple_of(to * share, share), share), :]
        top = jnp.max(jnp.abs(value), axis=0, keepdims=True)
        up, number = coded(value, top)
        p_send[to, 0:share, :] = word_of(number.astype(I32))
        p_send[to, share : share + 1, :] = up[:, :HALF]
        p_send[to, share + 1 : share + 2, :] = up[:, HALF:]

        @pl.when(t < COLS)
        def _():
            pltpu.make_async_remote_copy(
                p_send.at[to], p_recv.at[col], r_send, r_recv,
                device_id=(row, to), device_id_type=MESH,
            ).start()

        return 0

    lax.fori_loop(1, COLS + 1, give, 0)
    self_p = pltpu.make_async_copy(p_send.at[col], p_recv.at[col], self_sem.at[1])
    self_p.start()
    self_p.wait()
    rest = pl.ds(0, COLS - 1)
    pltpu.make_async_copy(p_recv.at[rest], p_recv.at[rest], r_recv).wait()

    def gain(n, totals):
        w = p_recv[n, 0:share, :]
        factor = power(p_recv[n, share : share + 2, :], 1) * LEAST
        a = totals[0] + (w >> 16).astype(F32) * factor[0:1, :]
        b = totals[1] + ((w << 16) >> 16).astype(F32) * factor[1:2, :]
        return a, b

    zero = jnp.zeros((share, HALF), F32)
    a, b = lax.fori_loop(0, COLS, gain, (zero, zero))

    top = jnp.max(jnp.maximum(jnp.abs(a), jnp.abs(b)), axis=0, keepdims=True)
    up, number_a = coded(a, top)
    number = jnp.concatenate([number_a, coded(b, top)[1]], axis=1)
    answer[:, SCAP : SCAP + 1, :] = jnp.broadcast_to(up.reshape(1, 1, HALF), (DEV, 1, HALF))
    high = jnp.floor(number * (1.0 / 256.0))
    low = (number - high * 256.0).astype(BF16)
    high = high.astype(BF16)
    for g in range(asks // HALF):
        chosen = take[:, g * HALF : (g + 1) * HALF]
        value = (tn(chosen, high) * 256.0 + tn(chosen, low)).astype(I32)
        word = word_of(value).reshape(HALF // span, span, HALF)
        answer[pl.ds(g * (HALF // span), HALF // span), 0:SCAP, :] = word[:, :SCAP, :]

    def send_answer(t, _):
        to = lax.rem(me + t * STRIDE, DEV)
        pltpu.make_async_remote_copy(
            answer.at[to], replies.at[me], a_send, a_recv,
            device_id=device_of(to), device_id_type=MESH,
        ).start()
        return 0

    lax.fori_loop(1, DEV, send_answer, 0)
    self_a = pltpu.make_async_copy(answer.at[me], replies.at[me], self_sem.at[2])
    self_a.start()

    for n in range(7):
        def left_here(j, _):
            at = piece(xpos, core, j)
            pltpu.make_async_copy(gathered.at[at], gathered.at[at], g_send.at[n, j]).wait()
            return 0

        lax.fori_loop(0, PIECES, left_here, 0)

    def written(n, _):
        write(n // CORES // PIECES, lax.rem(n // PIECES, CORES), lax.rem(n, PIECES)).wait()
        return 0

    lax.fori_loop(0, ROWS * PIECES, written, 0)
    rest = pl.ds(0, DEV - 1)
    pltpu.make_async_copy(send.at[rest], send.at[rest], v_send).wait()
    rest = pl.ds(0, COLS - 1)
    pltpu.make_async_copy(p_send.at[rest], p_send.at[rest], r_send).wait()
    self_a.wait()
    rest = pl.ds(0, DEV - 1)
    pltpu.make_async_copy(replies.at[rest], replies.at[rest], a_recv).wait()
    pltpu.make_async_copy(answer.at[rest], answer.at[rest], a_send).wait()


def emit_kernel(charge, replies, sowner, charge_now, drops, block, in_sem, out_sem):
    span = charge.shape[0] // 8

    def load(part):
        at = pl.ds(part * span, span)
        return pltpu.make_async_copy(charge.at[at], block.at[at], in_sem.at[part])

    def save(part):
        at = pl.ds(part * span, span)
        return pltpu.make_async_copy(block.at[at], charge_now.at[at], out_sem.at[part])

    for part in range(8):
        load(part).start()
    s_own = sowner[...]
    s_from, s_to = s_own[0:1, :], s_own[1:2, :]
    _, _, s_0, s_1 = ranks_of(s_from, s_to)
    wide = 2 * SCAP
    asks = DEV * wide
    line = iota((asks, s_own.shape[1]), 0)
    gate = (line == s_from * wide + s_0).astype(F32) - (line == s_to * wide + s_1).astype(F32)
    gate = gate.astype(BF16)
    for part in range(8):
        load(part).wait()
        save(part).start()
    w = replies[:, 0:SCAP, :]
    up = replies[:, SCAP : SCAP + 1, :].reshape(DEV, HALF)
    factor = (power(up, 1) * LEAST).reshape(DEV, 1, HALF)
    for half in range(2):
        number = (w >> 16) if half == 0 else ((w << 16) >> 16)
        value = number.astype(F32) * factor
        value = jnp.concatenate([value, value], axis=1).reshape(asks, HALF)
        high, low = split(value)
        drops[:, half * HALF : (half + 1) * HALF] = tn(gate, high) + tn(gate, low)
    for part in range(8):
        save(part).wait()


def emit(charge, replies, sowner):
    vmem, hbm = pl.BlockSpec(memory_space=pltpu.VMEM), pl.BlockSpec(memory_space=pl.ANY)
    dma = pltpu.SemaphoreType.DMA
    return pl.pallas_call(
        emit_kernel,
        out_shape=(
            jax.ShapeDtypeStruct(charge.shape, BF16),
            jax.ShapeDtypeStruct((sowner.shape[1], EXC), F32),
        ),
        in_specs=[hbm, vmem, vmem],
        out_specs=(hbm, vmem),
        scratch_shapes=[pltpu.VMEM(charge.shape, BF16), dma((8,)), dma((8,))],
        compiler_params=pltpu.CompilerParams(vmem_limit_bytes=FULL),
        name="emit",
    )(charge, replies, sowner)


def split(value):
    top = value.astype(BF16)
    return top, (value - top.astype(F32)).astype(BF16)


def step(cur, owner, slot, sowner, soffset, hist, coef, delays):
    hbm = pl.BlockSpec(memory_space=pl.ANY)
    nodes, rows = hist.shape[1], coef.shape[0]
    width = 2 * BLK
    dma = pltpu.SemaphoreType.DMA
    asks = DEV * 2 * SCAP
    return pl.pallas_call(
        step_kernel,
        out_shape=(
            jax.ShapeDtypeStruct((nodes, EXC), BF16),
            jax.ShapeDtypeStruct((DEV, SCAP + 1, HALF), I32),
        ),
        in_specs=[hbm] * 8,
        out_specs=(hbm, hbm),
        scratch_shapes=[
            pltpu.VMEM(cur.shape, F32),
            pltpu.VMEM(owner.shape, I32),
            pltpu.VMEM(slot.shape, I32),
            pltpu.VMEM(sowner.shape, I32),
            pltpu.VMEM(soffset.shape, I32),
            pltpu.SMEM(delays.shape, I32),
            pltpu.VMEM((DEV, CAP + 1, HALF), I32),
            pltpu.VMEM((DEV, CAP + 1, HALF), I32),
            pltpu.VMEM((SLOTS, 2 * EXC), BF16),
            pltpu.VMEM((BRANCH, EXC), BF16),
            pltpu.VMEM((BRANCH, EXC), BF16),
            pltpu.VMEM((OWN, EXC), BF16),
            pltpu.VMEM((nodes // width, rows, width), BF16),
            pltpu.VMEM(hist.shape, BF16),
            pltpu.VMEM((rows, EXC), F32),
            pltpu.VMEM((nodes, EXC), BF16),
            pltpu.VMEM((rows // COLS, asks), BF16),
            pltpu.VMEM((COLS, rows // COLS + 2, HALF), I32),
            pltpu.VMEM((COLS, rows // COLS + 2, HALF), I32),
            pltpu.VMEM((DEV, SCAP + 1, HALF), I32),
            dma((6,)), dma, dma, dma((3,)), dma, dma, dma((nodes // width,)), dma((ROWS, PIECES)),
            dma((7, PIECES)), dma((3, PIECES)), dma((4, PIECES)),
            dma, dma, dma, dma,
        ],
        compiler_params=pltpu.CompilerParams(
            collective_id=0, has_side_effects=True, vmem_limit_bytes=FULL
        ),
        name="step",
    )(cur, owner, slot, sowner, soffset, hist, coef, delays)


def local(
    currents, branch_owner, branch_slot, history, coefficients, delays, slab_owner, slab_offset
):
    sowner = slab_owner.T
    charge, replies = step(
        currents, branch_owner.T, branch_slot.T, sowner, slab_offset.T, history, coefficients, delays
    )
    return emit(charge, replies, sowner)


def solution(mesh):
    placed = (
        P(("row", "col"), None),
        P(("row", "col"), None),
        P(("row", "col"), None),
        P(None, "col", None),
        P("row", "col"),
        P("row", "col"),
        P(("row", "col"), None),
        P(("row", "col"), None),
    )
    return jax.shard_map(
        local,
        mesh=mesh,
        in_specs=placed,
        out_specs=(P("col", None), P(("row", "col"), None)),
        check_vma=False,
    )
```

time: 78.9 us -> 73.2 us (0.928)
  local copies, waits for them, and re-layouts: 9.44 us -> 0 us
  Pallas kernels: 68.4 us -> 72.4 us
    unnamed x14 -> x0, local copies, waits for them, and re-layouts: 9.44 us -> none
    pallas_call x0 -> x1, Pallas kernels: none -> 5.56 us  [emit(): pl.pallas_call(emit_kernel, out_shape=(jax.ShapeDtypeStruct(charge.shape,...]
    pallas_call x1, Pallas kernels: 68.4 us -> 66.8 us  [step(): pl.pallas_call(step_kernel, out_shape=(jax.ShapeDtypeStruct((nodes, EXC),...]
where the time goes in v3:
time: 73.2 us; the launch traced here: 73 us
  Pallas kernels  72.4 us (99%)
    pallas_call x1, Pallas kernels, step(): pl.pallas_call(step_kernel, out_shape=(jax.ShapeDtypeStruct((nodes, EXC),...  66.8 us
    pallas_call x1, Pallas kernels, emit(): pl.pallas_call(emit_kernel, out_shape=(jax.ShapeDtypeStruct(charge.shape,...  5.56 us

profile of v3, /device:TPU:1, one launch (start us, length us, event | category | flops | bytes accessed | tf_op | source)
XLA Modules:
  0.0 73.0 jit_solution(15102623724438554846)
XLA Ops:
  0.6 66.8 %step.1 = (bf16[8192,256]{1,0:T(8,128)(2,1)}, s32[128,5,128]{2,1,0:T(8,128)}) custom-call(f32[256,256]{1,0:T(8,128)} %cur_h.1, s32[2,256]{1,0:T(2,128)} %bitcast.6, s32[2,256]{1,0:T(2,128)} %bitcast.7, s32[2,64]{1,0:T(2,128)} %bitcast.4, s32[2,64]{1,0:T(2,128)} %bitcast.8, bf16[4,8192,256]{2,1,0:T(8,128)(2,1)} %hist.1, bf16[512,8192]{1,0:T(8,128)(2,1)} %coef_h.1, ...), custom_call_target="tpu_custom_call" | custom-call | tf_op jit(solution)/shard_map/step/pallas_call | solution.py:516
  67.5 5.6 %emit.1 = (bf16[8192,256]{1,0:T(8,128)(2,1)}, f32[64,256]{1,0:T(8,128)}) custom-call(bf16[8192,256]{1,0:T(8,128)(2,1)} %get-tuple-element.4.charge, s32[128,5,128]{2,1,0:T(8,128)} %get-tuple-element.5.replies, s32[2,64]{1,0:T(2,128)} %bitcast.5), custom_call_target="tpu_custom_call" | custom-call | tf_op jit(solution)/shard_map/emit/pallas_call | solution.py:491

commit v4 on v3

--- a/solution.py
+++ b/solution.py
@@ -86,15 +86,21 @@
     return a.astype(BF16), b.astype(BF16), rank_a, rank_b
 
 
-def greet(me):
+def greet(row, col):
     barrier = pltpu.get_barrier_semaphore()
 
-    def signal(t, _):
-        other = lax.rem(me + t, DEV)
-        pl.semaphore_signal(barrier, inc=1, device_id=device_of(other), device_id_type=MESH)
-        return 0
-
-    lax.fori_loop(1, DEV, signal, 0)
+    def down(t, _):
+        there = (lax.rem(row + t, ROWS), col)
+        pl.semaphore_signal(barrier, inc=1, device_id=there, device_id_type=MESH)
+        return 0
+
+    def along(t, _):
+        there = (row, lax.rem(col + t, COLS))
+        pl.semaphore_signal(barrier, inc=1, device_id=there, device_id_type=MESH)
+        return 0
+
+    lax.fori_loop(1, ROWS, down, 0)
+    lax.fori_loop(1, COLS, along, 0)
     return barrier
 
 
@@ -105,11 +111,11 @@
     send, recv, planes, q_hi, q_lo, past, coef, held, acc, gathered,
     take, p_send, p_recv, answer,
     first_sem, v_send, v_recv, self_sem, past_sem, h_sem, c_sem, w_sem,
-    g_send, g_near, g_pair, r_send, r_recv, a_send, a_recv,
+    g_send, g_near, g_pair, r_send, r_recv, a_send, a_recv, ready,
 ):
     row, col = lax.axis_index("row"), lax.axis_index("col")
     me = row * COLS + col
-    barrier = greet(me)
+    barrier = greet(row, col)
     small = ((cur_h, cur), (owner_h, owner), (slot_h, slot), (sowner_h, sowner), (soffset_h, soffset), (delays_h, delays))
     small = [pltpu.make_async_copy(a, b, first_sem.at[n]) for n, (a, b) in enumerate(small)]
     for copy in small:
@@ -192,9 +198,16 @@
         send[pl.ds(t * (chunk // CAP), chunk // CAP), 0:CAP, :] = word
         return 0
 
+    pl.semaphore_wait(barrier, ROWS - 1 + COLS - 1)
+
+    def pass_on(t, _):
+        there = (lax.rem(row + t, ROWS), col)
+        pl.semaphore_signal(ready, inc=1, device_id=there, device_id_type=MESH)
+        return 0
+
+    lax.fori_loop(1, ROWS, pass_on, 0)
     lax.fori_loop(0, SLOTS // chunk, fill, 0)
-
-    pl.semaphore_wait(barrier, DEV - 1)
+    pl.semaphore_wait(ready, ROWS - 1)
 
     def out(t, _):
         other = lax.rem(me + t * STRIDE, DEV)
@@ -448,7 +461,9 @@
     pltpu.make_async_copy(answer.at[rest], answer.at[rest], a_send).wait()
 
 
-def emit_kernel(charge, replies, sowner, charge_now, drops, block, in_sem, out_sem):
+def emit_kernel(
+    charge, replies_h, sowner_h, charge_now, drops, block, replies, sowner, in_sem, out_sem, small_sem
+):
     span = charge.shape[0] // 8
 
     def load(part):
@@ -459,8 +474,13 @@
         at = pl.ds(part * span, span)
         return pltpu.make_async_copy(block.at[at], charge_now.at[at], out_sem.at[part])
 
+    few = pltpu.make_async_copy(sowner_h, sowner, small_sem.at[0])
+    told = pltpu.make_async_copy(replies_h, replies, small_sem.at[1])
+    few.start()
     for part in range(8):
         load(part).start()
+    told.start()
+    few.wait()
     s_own = sowner[...]
     s_from, s_to = s_own[0:1, :], s_own[1:2, :]
     _, _, s_0, s_1 = ranks_of(s_from, s_to)
@@ -472,6 +492,7 @@
     for part in range(8):
         load(part).wait()
         save(part).start()
+    told.wait()
     w = replies[:, 0:SCAP, :]
     up = replies[:, SCAP : SCAP + 1, :].reshape(DEV, HALF)
     factor = (power(up, 1) * LEAST).reshape(DEV, 1, HALF)
@@ -494,9 +515,14 @@
             jax.ShapeDtypeStruct(charge.shape, BF16),
             jax.ShapeDtypeStruct((sowner.shape[1], EXC), F32),
         ),
-        in_specs=[hbm, vmem, vmem],
+        in_specs=[hbm, hbm, hbm],
         out_specs=(hbm, vmem),
-        scratch_shapes=[pltpu.VMEM(charge.shape, BF16), dma((8,)), dma((8,))],
+        scratch_shapes=[
+            pltpu.VMEM(charge.shape, BF16),
+            pltpu.VMEM(replies.shape, I32),
+            pltpu.VMEM(sowner.shape, I32),
+            dma((8,)), dma((8,)), dma((2,)),
+        ],
         compiler_params=pltpu.CompilerParams(vmem_limit_bytes=FULL),
         name="emit",
     )(charge, replies, sowner)
@@ -544,7 +570,7 @@
             pltpu.VMEM((DEV, SCAP + 1, HALF), I32),
             dma((6,)), dma, dma, dma((3,)), dma, dma, dma((nodes // width,)), dma((ROWS, PIECES)),
             dma((7, PIECES)), dma((3, PIECES)), dma((4, PIECES)),
-            dma, dma, dma, dma,
+            dma, dma, dma, dma, pltpu.SemaphoreType.REGULAR,
         ],
         compiler_params=pltpu.CompilerParams(
             collective_id=0, has_side_effects=True, vmem_limit_bytes=FULL

time: 73.2 us -> 72 us (0.984)
  Pallas kernels: 72.4 us -> 71.2 us
    pallas_call x1, Pallas kernels: 5.56 us -> 4.79 us  [emit(): pl.pallas_call(emit_kernel, out_shape=(jax.ShapeDtypeStruct(charge.shape,...]
where the time goes in v4:
time: 72 us; the launch traced here: 71.8 us
  Pallas kernels  71.2 us (99%)
    pallas_call x1, Pallas kernels, step(): pl.pallas_call(step_kernel, out_shape=(jax.ShapeDtypeStruct((nodes, EXC),...  66.4 us
    pallas_call x1, Pallas kernels, emit(): pl.pallas_call(emit_kernel, out_shape=(jax.ShapeDtypeStruct(charge.shape,...  4.79 us

profile of v4, /device:TPU:1, one launch (start us, length us, event | category | flops | bytes accessed | tf_op | source)
XLA Modules:
  0.0 71.8 jit_solution(4129222222140724294)
XLA Ops:
  0.6 66.4 %step.1 = (bf16[8192,256]{1,0:T(8,128)(2,1)}, s32[128,5,128]{2,1,0:T(8,128)}) custom-call(f32[256,256]{1,0:T(8,128)} %cur_h.1, s32[2,256]{1,0:T(2,128)} %bitcast.6, s32[2,256]{1,0:T(2,128)} %bitcast.7, s32[2,64]{1,0:T(2,128)} %bitcast.4, s32[2,64]{1,0:T(2,128)} %bitcast.8, bf16[4,8192,256]{2,1,0:T(8,128)(2,1)} %hist.1, bf16[512,8192]{1,0:T(8,128)(2,1)} %coef_h.1, ...), custom_call_target="tpu_custom_call" | custom-call | tf_op jit(solution)/shard_map/step/pallas_call | solution.py:542
  67.1 4.8 %emit.1 = (bf16[8192,256]{1,0:T(8,128)(2,1)}, f32[64,256]{1,0:T(8,128)}) custom-call(bf16[8192,256]{1,0:T(8,128)(2,1)} %get-tuple-element.4.charge, s32[128,5,128]{2,1,0:T(8,128)} %get-tuple-element.5.replies_h, s32[2,64]{1,0:T(2,128)} %bitcast.5), custom_call_target="tpu_custom_call" | custom-call | tf_op jit(solution)/shard_map/emit/pallas_call | solution.py:512

commit v5 on v4

--- a/solution.py
+++ b/solution.py
@@ -263,13 +263,6 @@
     weight = jnp.where(weight > 0, power(weight - 1, -1) * 2.0**-12, 0.0)
 
     share = acc.shape[0] // COLS
-    expand = ((iota((DEV, asks), 1) >> 3) == iota((DEV, asks), 0)).astype(BF16)
-    wide = tn(heard, expand)[48:56, :]
-    line = iota((span, asks), 0)
-    mine = line == (iota((span, asks), 1) & (span - 1))
-    place = jnp.sum(jnp.where(mine, wide, 0.0), axis=0, keepdims=True).astype(I32)
-    take[...] = (iota((share, asks), 0) == place).astype(BF16)
-
     def unpack(t, _):
         at = pl.ds(pl.multiple_of(t * chunk, chunk), chunk)
         w = recv[pl.ds(t * (chunk // CAP), chunk // CAP), 0:CAP, :].reshape(chunk, HALF)
@@ -332,6 +325,13 @@
 
     lax.fori_loop(0, PIECES, settle, 0)
 
+    expand = ((iota((DEV, asks), 1) >> 3) == iota((DEV, asks), 0)).astype(BF16)
+    wide = tn(heard, expand)[48:56, :]
+    line = iota((span, asks), 0)
+    mine = line == (iota((span, asks), 1) & (span - 1))
+    place = jnp.sum(jnp.where(mine, wide, 0.0), axis=0, keepdims=True).astype(I32)
+    take[...] = (iota((share, asks), 0) == place).astype(BF16)
+
     def near(t, _):
         j = turn(t)
         arrived(left, core, j, g_near.at[0, j])
@@ -420,21 +420,30 @@
     high = jnp.floor(number * (1.0 / 256.0))
     low = (number - high * 256.0).astype(BF16)
     high = high.astype(BF16)
-    for g in range(asks // HALF):
-        chosen = take[:, g * HALF : (g + 1) * HALF]
+
+    def reply(t, _):
+        g = lax.rem(row + t, ROWS)
+        chosen = take[:, pl.ds(pl.multiple_of(g * HALF, HALF), HALF)]
         value = (tn(chosen, high) * 256.0 + tn(chosen, low)).astype(I32)
-        word = word_of(value).reshape(HALF // span, span, HALF)
-        answer[pl.ds(g * (HALF // span), HALF // span), 0:SCAP, :] = word[:, :SCAP, :]
-
-    def send_answer(t, _):
-        to = lax.rem(me + t * STRIDE, DEV)
-        pltpu.make_async_remote_copy(
-            answer.at[to], replies.at[me], a_send, a_recv,
-            device_id=device_of(to), device_id_type=MESH,
-        ).start()
-        return 0
-
-    lax.fori_loop(1, DEV, send_answer, 0)
+        word = word_of(value).reshape(COLS, span, HALF)
+        answer[pl.ds(g * COLS, COLS), 0:SCAP, :] = word[:, :SCAP, :]
+
+        def send_answer(n, _):
+            to = g * COLS + lax.rem(col + n, COLS)
+
+            @pl.when(to != me)
+            def _():
+                pltpu.make_async_remote_copy(
+                    answer.at[to], replies.at[me], a_send, a_recv,
+                    device_id=device_of(to), device_id_type=MESH,
+                ).start()
+
+            return 0
+
+        lax.fori_loop(0, COLS, send_answer, 0)
+        return 0
+
+    lax.fori_loop(0, asks // HALF, reply, 0)
     self_a = pltpu.make_async_copy(answer.at[me], replies.at[me], self_sem.at[2])
     self_a.start()
 

time: 72 us -> 73.6 us (1.022)
  Pallas kernels: 71.2 us -> 72.8 us
    pallas_call x1, Pallas kernels: 66.4 us -> 68 us  [step(): pl.pallas_call(step_kernel, out_shape=(jax.ShapeDtypeStruct((nodes, EXC),...]
where the time goes in v5:
time: 73.6 us; the launch traced here: 73.4 us
  Pallas kernels  72.8 us (99%)
    pallas_call x1, Pallas kernels, step(): pl.pallas_call(step_kernel, out_shape=(jax.ShapeDtypeStruct((nodes, EXC),...  68 us
    pallas_call x1, Pallas kernels, emit(): pl.pallas_call(emit_kernel, out_shape=(jax.ShapeDtypeStruct(charge.shape,...  4.79 us

profile of v5, /device:TPU:1, one launch (start us, length us, event | category | flops | bytes accessed | tf_op | source)
XLA Modules:
  0.0 73.4 jit_solution(2186816998961972989)
XLA Ops:
  0.6 68.0 %step.1 = (bf16[8192,256]{1,0:T(8,128)(2,1)}, s32[128,5,128]{2,1,0:T(8,128)}) custom-call(f32[256,256]{1,0:T(8,128)} %cur_h.1, s32[2,256]{1,0:T(2,128)} %bitcast.6, s32[2,256]{1,0:T(2,128)} %bitcast.7, s32[2,64]{1,0:T(2,128)} %bitcast.4, s32[2,64]{1,0:T(2,128)} %bitcast.8, bf16[4,8192,256]{2,1,0:T(8,128)(2,1)} %hist.1, bf16[512,8192]{1,0:T(8,128)(2,1)} %coef_h.1, ...), custom_call_target="tpu_custom_call" | custom-call | tf_op jit(solution)/shard_map/step/pallas_call | solution.py:551
  68.6 4.8 %emit.1 = (bf16[8192,256]{1,0:T(8,128)(2,1)}, f32[64,256]{1,0:T(8,128)}) custom-call(bf16[8192,256]{1,0:T(8,128)(2,1)} %get-tuple-element.4.charge, s32[128,5,128]{2,1,0:T(8,128)} %get-tuple-element.5.replies_h, s32[2,64]{1,0:T(2,128)} %bitcast.5), custom_call_target="tpu_custom_call" | custom-call | tf_op jit(solution)/shard_map/emit/pallas_call | solution.py:521

commit v6 on v4

--- a/solution.py
+++ b/solution.py
@@ -263,13 +263,6 @@
     weight = jnp.where(weight > 0, power(weight - 1, -1) * 2.0**-12, 0.0)
 
     share = acc.shape[0] // COLS
-    expand = ((iota((DEV, asks), 1) >> 3) == iota((DEV, asks), 0)).astype(BF16)
-    wide = tn(heard, expand)[48:56, :]
-    line = iota((span, asks), 0)
-    mine = line == (iota((span, asks), 1) & (span - 1))
-    place = jnp.sum(jnp.where(mine, wide, 0.0), axis=0, keepdims=True).astype(I32)
-    take[...] = (iota((share, asks), 0) == place).astype(BF16)
-
     def unpack(t, _):
         at = pl.ds(pl.multiple_of(t * chunk, chunk), chunk)
         w = recv[pl.ds(t * (chunk // CAP), chunk // CAP), 0:CAP, :].reshape(chunk, HALF)
@@ -331,6 +324,13 @@
         return 0
 
     lax.fori_loop(0, PIECES, settle, 0)
+
+    expand = ((iota((DEV, asks), 1) >> 3) == iota((DEV, asks), 0)).astype(BF16)
+    wide = tn(heard, expand)[48:56, :]
+    line = iota((span, asks), 0)
+    mine = line == (iota((span, asks), 1) & (span - 1))
+    place = jnp.sum(jnp.where(mine, wide, 0.0), axis=0, keepdims=True).astype(I32)
+    take[...] = (iota((share, asks), 0) == place).astype(BF16)
 
     def near(t, _):
         j = turn(t)

time: 72 us -> 71.9 us (level)
  no operation moved by 1% of the time
where the time goes in v6:
time: 71.9 us; the launch traced here: 71.7 us
  Pallas kernels  71.1 us (99%)
    pallas_call x1, Pallas kernels, step(): pl.pallas_call(step_kernel, out_shape=(jax.ShapeDtypeStruct((nodes, EXC),...  66.3 us
    pallas_call x1, Pallas kernels, emit(): pl.pallas_call(emit_kernel, out_shape=(jax.ShapeDtypeStruct(charge.shape,...  4.79 us

profile of v6, /device:TPU:1, one launch (start us, length us, event | category | flops | bytes accessed | tf_op | source)
XLA Modules:
  0.0 71.7 jit_solution(4162890188860081546)
XLA Ops:
  0.6 66.3 %step.1 = (bf16[8192,256]{1,0:T(8,128)(2,1)}, s32[128,5,128]{2,1,0:T(8,128)}) custom-call(f32[256,256]{1,0:T(8,128)} %cur_h.1, s32[2,256]{1,0:T(2,128)} %bitcast.6, s32[2,256]{1,0:T(2,128)} %bitcast.7, s32[2,64]{1,0:T(2,128)} %bitcast.4, s32[2,64]{1,0:T(2,128)} %bitcast.8, bf16[4,8192,256]{2,1,0:T(8,128)(2,1)} %hist.1, bf16[512,8192]{1,0:T(8,128)(2,1)} %coef_h.1, ...), custom_call_target="tpu_custom_call" | custom-call | tf_op jit(solution)/shard_map/step/pallas_call | solution.py:542
  67.0 4.8 %emit.1 = (bf16[8192,256]{1,0:T(8,128)(2,1)}, f32[64,256]{1,0:T(8,128)}) custom-call(bf16[8192,256]{1,0:T(8,128)(2,1)} %get-tuple-element.4.charge, s32[128,5,128]{2,1,0:T(8,128)} %get-tuple-element.5.replies_h, s32[2,64]{1,0:T(2,128)} %bitcast.5), custom_call_target="tpu_custom_call" | custom-call | tf_op jit(solution)/shard_map/emit/pallas_call | solution.py:512
